TPU v7x, 128 devices: a whole 4x4x4 slice. The times are simulated.
128 devices in a mesh: lon: 16 (over x, z_lo, core), lat: 8 (over z_hi, y).
Axes of the slice: x: 4, y: 4, z: 4 (z_hi: 2, z_lo: 2; z = z_hi * 2 + z_lo), core: 2. Of those that a mesh axis runs over, the one named last changes fastest.
Arguments:
- background: float32 [5, 32, 256, 2048], P(None, None, 'lat', 'lon'), may hold values from -6 to 6
- velocity: float32 [2, 32, 256, 2048], P(None, None, 'lat', 'lon'), may hold values from -0.22 to 0.22
- diffusivity: float32 [5], replicated, may hold values from 0.02 to 0.12
- obs_value: float32 [131072], P(('lon', 'lat')), may hold values from -6 to 6
- obs_weight: float32 [131072], P(('lon', 'lat')), may hold values from 0.25 to 4
- obs_owner: int32 [131072, 1], P(('lon', 'lat')), may hold values from 0 to 127; in each aligned block of 1024 rows (0 to 1023, 1024 to 2047, ...) at most 16 rows name the same one
- obs_counts: int32 [128, 8], P(('lon', 'lat')), may hold values from 1 to 128, 768 in all within a row
- obs_cell: int32 [131072], P(('lon', 'lat')), may hold values from 0 to 655359
Outputs:
- forecast: float32 [5, 32, 256, 2048], P(None, None, 'lat', 'lon')
- adjoint_state: float32 [5, 32, 256, 2048], P(None, None, 'lat', 'lon')
- departures: float32 [131072], P(('lon', 'lat'))
Inputs may be any that keep to these rules, and one draw needn't show every extreme that they name: `obs_owner`: among the rows of one device, padding rows included, no slab is named more than 16 times, a bound that some block reaches. `obs_counts`: each device's 8 counts sum to 768; one of them is 128. `obs_cell`: index into the owner's slab, flattened over field, level, row and longitude.
All inputs are finite; a program needn't handle non-finite values.
Results may differ from a plain program's by a relative error of at most 0.00012.
Values sent between devices are 32-bit elements; how exact they have to be, the bound alone decides.
No kernel may reach another device: no remote copies, remote signals or barrier semaphores. Data moves between devices by JAX's collectives and lax.ppermute only.
A program may use at most 128 MiB of HBM per device.

v0:
```python
import jax
import jax.numpy as jnp
from jax import lax
from jax.experimental import pallas as pl
from jax.experimental.pallas import tpu as pltpu
from jax.sharding import PartitionSpec as P


STEPS = 2
F = 5
K = 32
CL = 32
CW = 128
PLANES = F * K
ALL = PLANES + 2 * K
EXT = 40
ROWS = PLANES * CL
NBLK = 8
NDEV = 128
CAP = 16
MIB = 1 << 20
f32 = jnp.float32
i32 = jnp.int32


V = pltpu.VMEM
S = pltpu.SMEM
H = pltpu.HBM


def iota(shape, dim):
    return lax.broadcasted_iota(i32, shape, dim)


def call(body, outs, ins, name, scratch=(), vmem=53, flops=10**6, nbytes=10**6):
    return pl.pallas_call(
        body,
        out_shape=[jax.ShapeDtypeStruct(shape, dtype) for shape, dtype, *_ in outs],
        in_specs=[pl.BlockSpec(memory_space=space) for space, _ in ins],
        out_specs=[pl.BlockSpec(memory_space=out[2] if len(out) > 2 else V) for out in outs],
        scratch_shapes=list(scratch),
        compiler_params=pltpu.CompilerParams(vmem_limit_bytes=vmem * MIB),
        cost_estimate=pl.CostEstimate(flops=flops, bytes_accessed=nbytes, transcendentals=0),
        name=name,
    )(*[x for _, x in ins])


def reverse_lanes(x):
    return jnp.take_along_axis(x, 127 - iota(x.shape, 1), axis=1)


def fold_sign(planes):
    kind = iota((planes, CW), 0) // K
    return jnp.where((kind == 2) | (kind == 3) | (kind >= F), -1.0, 1.0).astype(f32)


def where_am_i():
    at = lax.axis_index("lat")
    return at & 1 == 1, at == lax.axis_size("lat") - 1, at == 0


def partners():
    i, j = lax.axis_index("lon"), lax.axis_index("lat")
    n, m = lax.axis_size("lon"), lax.axis_size("lat")
    top = j == m - 1
    to_east, to_west = lax.rem(i + 1, n), lax.rem(i + n - 1, n)
    north_of, south_of = jnp.minimum(j + 1, m - 1), jnp.maximum(j - 1, 0)
    return (
        jnp.where(top, lax.rem(2 * n - 2 - i, n), to_east) * m + north_of,
        jnp.where(top, lax.rem(n - i, n), to_west) * m + north_of,
        to_east * m + south_of,
        to_west * m + south_of,
    )


def corner_rows(blocks, line, place):
    slot = iota((8, CW), 1) & 3
    rows = []
    for start in range(0, len(blocks), 4):
        row = jnp.zeros((8, CW), f32)
        for kind, block in enumerate(blocks[start : start + 4]):
            row = jnp.where(slot == kind, pltpu.roll(block, (kind - place) % CW, axis=1), row)
        rows.append(row[line : line + 1])
    return rows


def post_corners(pay, rows, bottom):
    for n, at in enumerate(partners()):
        for r in range(2):
            @pl.when(jnp.logical_not(bottom) if n >= 2 else at >= 0)
            def _(n=n, at=at, r=r):
                pay[pl.ds(MESSAGE * at + 1 + r, 1), :] = rows[n][r]


def corner_line(got, kind, first, second):
    slot = iota((8, CW), 1) & 3
    ats = partners()
    line = jnp.zeros((8, CW), f32)
    for place, n in ((1, first), (2, second)):
        row = got[pl.ds(MESSAGE * ats[n] + 1 + kind // 4, 1), :]
        moved = pltpu.roll(jnp.broadcast_to(row, (8, CW)), (place - kind % 4) % CW, axis=1)
        line = jnp.where(slot == place, moved, line)
    return line[:1]


NE, NW, SE, SW = range(4)
MESSAGE = 3
FLIPPED = (2, 3, 5, 6)


def thirds(x):
    pieces = []
    for _ in range(3):
        piece = x.astype(jnp.bfloat16)
        pieces.append(piece)
        x = x - piece.astype(f32)
    return pieces


def edges_kernel(x, vel, own, pay1, pay2, held, sems):
    odd, top, _ = where_am_i()
    copies = []
    for kind in range(F + 2):
        ref, plane = (x, kind * K) if kind < F else (vel, (kind - F) * K)
        copies.append(
            pltpu.make_async_copy(
                ref.at[pl.ds(plane * CL, K * CL)],
                held.at[pl.ds(kind * K * CL, K * CL)],
                sems.at[kind],
            )
        )
    for copy in copies:
        copy.start()
    group = iota((CL, CW), 1) >> 2
    for kind in range(F + 2):
        copies[kind].wait()
        for d in range(2 if kind < F else 1):
            low = held[pl.ds(kind * K * CL + d, K, stride=CL), :]
            high = held[pl.ds(kind * K * CL + CL - 1 - d, K, stride=CL), :]
            to = slice(d * ALL + kind * K, d * ALL + kind * K + K)
            pay1[to, :] = jnp.where(odd, low, high)
            pay2[to, :] = jnp.where(odd, high, low)

        def step(level, packed):
            rows = held[pl.ds(pl.multiple_of((kind * K + level) * CL, CL), CL), :]
            moved = pltpu.roll(rows, 4 * level + 2, axis=1)
            return jnp.where(group == level, moved, packed)

        own[kind] = lax.fori_loop(0, K, step, jnp.zeros((CL, CW), f32), unroll=True)

    @pl.when(top)
    def _():
        pay2[:ALL, :] = fold_sign(ALL) * reverse_lanes(pay2[:ALL, :])
        pay2[ALL:, :] = fold_sign(PLANES) * reverse_lanes(pay2[ALL:, :])


def halo_rows(got1, got2, odd):
    near, far = slice(0, ALL), slice(ALL, ALL + PLANES)
    norths = [jnp.where(odd, got2[cut, :], got1[cut, :]) for cut in (near, far)]
    souths = [jnp.where(odd, got1[cut, :], got2[cut, :]) for cut in (near, far)]
    return norths + souths


def spread(line):
    level, lane = iota((K, CW), 0), iota((K, CW), 1)
    return jnp.take_along_axis(
        jnp.broadcast_to(line, (K, CW)), (lane + 4 * level + 2) & (CW - 1), axis=1
    )


def gather_line(rows):
    level, lane = iota((K, CW), 0), iota((K, CW), 1)
    moved = jnp.take_along_axis(rows, (lane - 4 * level - 2) & (CW - 1), axis=1)
    return jnp.sum(jnp.where(lane >> 2 == level, moved, 0.0), axis=0, keepdims=True)


def north(x):
    return pltpu.roll(x, EXT - 1, axis=0)


def south(x):
    return pltpu.roll(x, 1, axis=0)


def east(x):
    return pltpu.roll(x, CW - 1, axis=1)


def west(x):
    return pltpu.roll(x, 1, axis=1)


def swapped(x, slot):
    return jnp.where(slot == 1, east(x), jnp.where(slot == 2, west(x), x))


def parts(u, v):
    return (
        1.0 - jnp.abs(u) - jnp.abs(v),
        -jnp.minimum(u, 0.0),
        jnp.maximum(u, 0.0),
        -jnp.minimum(v, 0.0),
        jnp.maximum(v, 0.0),
    )


def pack_kernel(counts, value, weight, owner, cell, own, pay, slots):
    dest = iota((NDEV, 128), 0)
    lane = iota((1, 128), 1)
    before = (iota((128, 128), 0) < iota((128, 128), 1)).astype(f32).astype(jnp.bfloat16)
    ones = jnp.ones((128, 128), jnp.bfloat16)
    carry = jnp.zeros((NDEV, 128), f32)
    total = jnp.zeros((NDEV, 128), f32)
    place = iota((CAP, 128), 0).astype(f32)
    for b in range(NBLK):
        live = lane < counts[0, b]
        who = jnp.where(live, owner[b : b + 1, :], -1)
        hot = (dest == who).astype(f32)
        hot16 = hot.astype(jnp.bfloat16)
        earlier = carry + jnp.dot(hot16, before, preferred_element_type=f32)
        carry = carry + jnp.dot(hot16, ones, preferred_element_type=f32)
        slot = jnp.sum(hot * earlier, axis=0, keepdims=True)
        slot = jnp.where(live, slot, -1.0)
        slots[b : b + 1, :] = slot
        code = (cell[b : b + 1, :] + (b % (STEPS + 1)) * (ROWS * CW)).astype(f32)
        here = place == slot
        fields = [
            jnp.where(here, data, 0.0) for data in (value[b : b + 1, :], weight[b : b + 1, :], code)
        ]
        fields.append(jnp.zeros((128 - 3 * CAP, 128), f32))
        total = total + lax.dot_general(
            jnp.concatenate([hot16] * 3, axis=1),
            jnp.concatenate(thirds(jnp.concatenate(fields, axis=0)), axis=1),
            (((1,), (1,)), ((), ())),
            preferred_element_type=f32,
        )
    pay[...] = jnp.zeros(pay.shape, f32)
    pay[pl.ds(0, NDEV, stride=MESSAGE), :] = total
    low = [own[kind, :8, :] for kind in range(F + 2)]
    high = [own[kind, CL - 8 :, :] for kind in range(F + 2)]
    _, _, bottom = where_am_i()
    post_corners(
        pay,
        [
            corner_rows(high, 7, 1),
            corner_rows(high, 7, 2),
            corner_rows(low, 0, 1),
            corner_rows(low, 0, 2),
        ],
        bottom,
    )


PAD = 8
GROUP = 8
UNROLL = 4
TILES = CL // 8


def core_kernel(kap, arrived, x, vel_in, got1, got2, own, from_west, from_east,
                replies, forecast, part, pay1, pay2, spill,
                states, forcing, vel, rows_of, adds, cell_of, index_v, index_s,
                halo, edge, side, mine_all, beside, beside1, own_f, own_a, sems):
    odd, top, bottom = where_am_i()
    load_x = pltpu.make_async_copy(x, states.at[pl.ds(PAD, ROWS)], sems.at[0])
    load_x.start()
    load_v = pltpu.make_async_copy(vel_in, vel.at[pl.ds(PAD, 2 * K * CL)], sems.at[1])
    load_v.start()
    box = arrived[pl.ds(0, NDEV, stride=MESSAGE), :]
    index_v[...] = (jnp.transpose(box)[2 * CAP : 3 * CAP].astype(i32) >> 7) + PAD
    load_i = pltpu.make_async_copy(index_v, index_s, sems.at[2])
    load_i.start()

    lane = iota((EXT, CW), 1)
    slot = lane & 3
    for n, rows in enumerate(halo_rows(got1, got2, odd)):
        halo[n, : rows.shape[0], :] = rows
    near_slot = iota((CL, CW), 1) & 3
    for kind in range(F + 2):
        side[kind, :CL, :] = jnp.where(near_slot < 2, from_west[kind], from_east[kind])
        side[kind, CL:, :] = jnp.zeros((8, CW), f32)
        mine_all[kind, :CL, :] = own[kind]
        mine_all[kind, CL:, :] = jnp.zeros((8, CW), f32)
        span = slice(kind * K, kind * K + K)
        mine_all[kind, CL : CL + 1, :] = gather_line(halo[0, span, :])
        mine_all[kind, EXT - 1 :, :] = gather_line(halo[2, span, :])
        line = corner_line(arrived, kind, NW, NE)
        side[kind, CL : CL + 1, :] = jnp.where(top, -line, line) if kind in FLIPPED else line
        line = corner_line(arrived, kind, SW, SE)
        side[kind, EXT - 1 :, :] = jnp.where(bottom, 0.0, line)
    base, um, up, vm, vp = parts(side[F], side[F + 1])
    for f in range(F):
        k = kap[f]
        mine = mine_all[f]
        near = side[f]
        e = jnp.where(slot == 1, east(mine), east(near))
        w = jnp.where(slot == 1, west(near), west(mine))
        beside[f] = swapped(near, slot)
        next_near = (
            (base - 4.0 * k) * near
            + (k + um) * e
            + (k + up) * w
            + (k + vm) * north(near)
            + (k + vp) * south(near)
        )
        beside1[f] = swapped(next_near, slot)

    @pl.loop(0, 3 * ROWS // 256)
    def _(i):
        forcing[pl.ds(pl.multiple_of(i * 256, 256) + PAD, 256), :] = jnp.zeros((256, CW), f32)

    first = iota((8, CW), 1) == 0
    last = iota((8, CW), 1) == CW - 1
    row0 = iota((8, CW), 0) == 0
    row7 = iota((8, CW), 0) == 7
    first_k = iota((K, CW), 1) == 0
    last_k = iota((K, CW), 1) == CW - 1
    NORTH, SOUTH = 0, 2
    load_x.wait()
    load_v.wait()

    def line(ref, row, f, base=0):
        return ref[pl.ds(PAD + base + f * K * CL + row, K, stride=CL), :]

    def span(f):
        return slice(f * K, f * K + K)

    for n, at, inner in ((NORTH, CL, CL - 1), (SOUTH, EXT - 1, 0)):
        base, um, up, vm, vp = parts(halo[n, span(F), :], halo[n, span(F + 1), :])
        for f in range(F):
            k = kap[f]
            a = halo[n, span(f), :]
            far = halo[n + 1, span(f), :]
            close = line(states, inner, f)
            to_north, to_south = (far, close) if n == NORTH else (close, far)
            h = spread(side[f, at : at + 1, :])
            b = (
                (base - 4.0 * k) * a
                + (k + um) * east(jnp.where(first_k, h, a))
                + (k + up) * west(jnp.where(last_k, h, a))
                + (k + vm) * to_north
                + (k + vp) * to_south
            )
            if n == SOUTH:
                b = jnp.where(bottom, 0.0, b)
            edge[n // 2, span(f), :] = b

    def around(ref, start, t, north_row, south_row):
        at = start + 8 * t
        a = ref[pl.ds(pl.multiple_of(at, 8), 8), :]
        n = ref[pl.ds(at + 1, 8), :]
        s = ref[pl.ds(at - 1, 8), :]
        if t == TILES - 1:
            n = jnp.where(row7, north_row, n)
        if t == 0:
            s = jnp.where(row0, south_row, s)
        return a, n, s

    def forward(source, target, packed, north_of, south_of):
        @pl.loop(0, K, unroll=UNROLL)
        def _(level):
            turn = 126 - 4 * level
            for t in range(TILES):
                at = pl.multiple_of(PAD + level * CL, 8) + 8 * t
                u = vel[pl.ds(pl.multiple_of(at, 8), 8), :]
                v = vel[pl.ds(pl.multiple_of(at + K * CL, 8), 8), :]
                base, um, up, vm, vp = parts(u, v)
                for f in range(F):
                    k = kap[f]
                    plane = f * K + level
                    start = PAD + source * ROWS + plane * CL
                    a, n, s = around(states, start, t, north_of(plane), south_of(plane))
                    h = pltpu.roll(packed[f, 8 * t : 8 * t + 8, :], turn, axis=1)
                    b = (
                        (base - 4.0 * k) * a
                        + (k + um) * jnp.where(last, h, east(a))
                        + (k + up) * jnp.where(first, h, west(a))
                        + (k + vm) * n
                        + (k + vp) * s
                    )
                    to = PAD + target * ROWS + plane * CL + 8 * t
                    states[pl.ds(pl.multiple_of(to, 8), 8), :] = b

    def halo_row(n):
        return lambda plane: halo[n, pl.ds(plane, 1), :]

    def edge_row(n):
        return lambda plane: edge[n, pl.ds(plane, 1), :]

    forward(0, 1, beside, halo_row(NORTH), halo_row(SOUTH))
    forward(1, 2, beside1, edge_row(0), edge_row(1))
    save = pltpu.make_async_copy(states.at[pl.ds(PAD + 2 * ROWS, ROWS)], forecast, sems.at[3])
    save.start()

    load_i.wait()

    @pl.loop(0, NDEV)
    def _(s):
        for q in range(CAP):
            at = index_s[q, s]
            rows_of[pl.ds(q * NDEV + s, 1), :] = states[pl.ds(at, 1), :]

    lane_s = iota((NDEV, CW), 1)
    cells = box.astype(i32)
    ones = jnp.ones((3 * CW, CW), jnp.bfloat16)
    modelled = jnp.zeros((NDEV, CW), f32)
    for q in range(CAP):
        cut = slice(q * NDEV, (q + 1) * NDEV)
        cell = jnp.broadcast_to(cells[:, 2 * CAP + q : 2 * CAP + q + 1], (NDEV, CW))
        cell_of[cut, :] = cell
        seen = jnp.where(lane_s == cell & (CW - 1), rows_of[cut, :], 0.0)
        seen = jnp.dot(
            jnp.concatenate(thirds(seen), axis=1), ones, preferred_element_type=f32
        )
        modelled = jnp.where(lane_s == q, seen, modelled)
    weight = pltpu.roll(box, CW - CAP, axis=1)
    result = jnp.where(lane_s < CAP, weight * (box - modelled), 0.0)
    replies[...] = jnp.zeros(replies.shape, f32)
    replies[pl.ds(0, NDEV, stride=MESSAGE), :] = result
    for start in range(0, CAP, GROUP):
        for q in range(start, start + GROUP):
            cut = slice(q * NDEV, (q + 1) * NDEV)
            dep = jnp.broadcast_to(result[:, q : q + 1], (NDEV, CW))
            adds[cut, :] = jnp.where(lane_s == cell_of[cut, :] & (CW - 1), dep, 0.0)
        for q in range(start + GROUP - 1, start, -1):
            cut = slice(q * NDEV, (q + 1) * NDEV)
            mine = cell_of[cut, :] >> 7
            acc = adds[cut, :]
            for p in range(start, q):
                other = slice(p * NDEV, (p + 1) * NDEV)
                acc = acc + jnp.where(mine == cell_of[other, :] >> 7, adds[other, :], 0.0)
            adds[cut, :] = acc

    @pl.loop(0, NDEV)
    def _(s):
        for start in range(0, CAP, GROUP):
            ats = [index_s[q, s] for q in range(start, start + GROUP)]
            olds = [forcing[pl.ds(at, 1), :] for at in ats]
            for n in range(GROUP):
                forcing[pl.ds(ats[n], 1), :] = (
                    olds[n] + adds[pl.ds((start + n) * NDEV + s, 1), :]
                )

    own_f[...] = jnp.zeros(own_f.shape, f32)
    own_a[...] = jnp.zeros(own_a.shape, f32)
    group = iota((8, CW), 1) >> 2

    @pl.loop(0, K, unroll=UNROLL)
    def _(level):
        here = group == level
        turn = 4 * level + 2
        for t in range(TILES):
            at = pl.multiple_of(PAD + level * CL, 8) + 8 * t
            u = vel[pl.ds(pl.multiple_of(at, 8), 8), :]
            v, vn, vs = around(vel, PAD + (K + level) * CL, t, 0.0, 0.0)
            base, um, up, _, _ = parts(u, v)
            vm = -jnp.minimum(vs, 0.0)
            vp = jnp.maximum(vn, 0.0)
            cut = slice(8 * t, 8 * t + 8)
            for f in range(F):
                k = kap[f]
                plane = f * K + level
                a, n, s = around(forcing, PAD + 2 * ROWS + plane * CL, t, 0.0, 0.0)
                own_f[f, cut, :] = jnp.where(here, pltpu.roll(a, turn, axis=1), own_f[f, cut, :])
                to = pl.ds(pl.multiple_of(PAD + ROWS + plane * CL + 8 * t, 8), 8)
                more = forcing[to, :]
                own_a[f, cut, :] = jnp.where(here, pltpu.roll(more, turn, axis=1), own_a[f, cut, :])
                b = (
                    (base - 4.0 * k) * a
                    + jnp.where(first, 0.0, west((k + um) * a))
                    + jnp.where(last, 0.0, east((k + up) * a))
                    + (k + vm) * s
                    + (k + vp) * n
                    + more
                )
                forcing[to, :] = b

    for n, at, inner in ((NORTH, CL, CL - 1), (SOUTH, EXT - 1, 0)):
        hu, hv = halo[n, span(F), :], halo[n, span(F + 1), :]
        base, um, up, vm, vp = parts(hu, hv)
        nearest = line(vel, inner, 1)
        push = jnp.maximum(nearest, 0.0) if n == SOUTH else -jnp.minimum(nearest, 0.0)
        on = vp if n == SOUTH else vm
        for f in range(F):
            k = kap[f]
            b = (k + push) * line(forcing, inner, f, 2 * ROWS)
            if n == SOUTH:
                b = jnp.where(bottom, 0.0, b)
            edge[n // 2, span(f), :] = b
            near = (
                (base - 4.0 * k) * b
                + jnp.where(first_k, 0.0, west((k + um) * b))
                + jnp.where(last_k, 0.0, east((k + up) * b))
                + (k + push) * line(forcing, inner, f, ROWS)
            )
            for d, rows in ((0, near), (1, (k + on) * b)):
                to = slice(d * PLANES + f * K, d * PLANES + f * K + K)
                mirrored = reverse_lanes(rows)
                mirrored = -mirrored if f in FLIPPED else mirrored
                if n == NORTH:
                    pay1[to, :] = rows
                    pay2[to, :] = jnp.where(top, mirrored, rows)
                else:
                    pay1[to, :] = jnp.where(odd, rows, pay1[to, :])
                    pay2[to, :] = jnp.where(odd, pay2[to, :], rows)

    base, um, up, vm, vp = parts(side[F], side[F + 1])
    obase, oum, oup, ovm, ovp = parts(mine_all[F], mine_all[F + 1])
    gone = bottom & (iota((EXT, CW), 0) >= CL + 2)
    ends = []
    for f in range(F):
        k = kap[f]
        a = own_f[f]
        oa, ob = (k + oum) * a, (k + oup) * a
        b = jnp.where(slot == 1, east(ob), jnp.where(slot == 2, west(oa), 0.0))
        a = (
            (obase - 4.0 * k) * a
            + jnp.where(slot == 1, west(oa), east(ob))
            + south((k + ovm) * a)
            + north((k + ovp) * a)
        )
        a = jnp.where(gone, 0.0, a) + own_a[f]
        pa = (k + um) * b
        pb = (k + up) * b
        beside1[f] = swapped(jnp.where(slot == 1, pa, pb), slot)
        inner = (
            (base - 4.0 * k) * b
            + south((k + vm) * b)
            + north((k + vp) * b)
            + jnp.where(slot == 1, east((k + oup) * a), west((k + oum) * a))
        )
        outer = jnp.where(slot == 0, east(pb), west(pa))
        beyond = jnp.where((slot == 1) | (slot == 2), inner, outer)
        spill[f] = beyond[:CL]
        ends.append(beyond[CL:])
    post_corners(
        replies,
        [
            corner_rows(ends, 0, 2),
            corner_rows(ends, 0, 1),
            corner_rows(ends, 7, 2),
            corner_rows(ends, 7, 1),
        ],
        bottom,
    )

    def step(level):
        turn = 126 - 4 * level
        for t in range(TILES):
            at = pl.multiple_of(PAD + level * CL, 8) + 8 * t
            u = vel[pl.ds(pl.multiple_of(at, 8), 8), :]
            v, vn, vs = around(
                vel,
                PAD + (K + level) * CL,
                t,
                halo[NORTH, pl.ds((F + 1) * K + level, 1), :],
                halo[SOUTH, pl.ds((F + 1) * K + level, 1), :],
            )
            base, um, up, _, _ = parts(u, v)
            vm = -jnp.minimum(vs, 0.0)
            vp = jnp.maximum(vn, 0.0)
            for f in range(F):
                k = kap[f]
                plane = f * K + level
                start = PAD + ROWS + plane * CL
                a, n, s = around(forcing, start, t, edge_row(0)(plane), edge_row(1)(plane))
                h = pltpu.roll(beside1[f, 8 * t : 8 * t + 8, :], turn, axis=1)
                b = (
                    (base - 4.0 * k) * a
                    + jnp.where(first, h, west((k + um) * a))
                    + jnp.where(last, h, east((k + up) * a))
                    + (k + vm) * s
                    + (k + vp) * n
                    + forcing[pl.ds(pl.multiple_of(PAD + plane * CL + 8 * t, 8), 8), :]
                )
                forcing[pl.ds(pl.multiple_of(PAD + plane * CL + 8 * t, 8), 8), :] = b

    saves = [save]
    for half in range(2):
        pl.loop(half * (K // 2), (half + 1) * (K // 2), unroll=UNROLL)(step)
        for f in range(F):
            at = f * K * CL + half * (K // 2) * CL
            size = K // 2 * CL
            saves.append(
                pltpu.make_async_copy(
                    forcing.at[pl.ds(PAD + at, size)],
                    part.at[pl.ds(at, size)],
                    sems.at[4 + half * F + f],
                )
            )
            saves[-1].start()
    for copy in saves:
        copy.wait()


def finish_kernel(part, from_west, from_east, got1, got2, returned, owner, slots,
                  adjoint, departures, held, sems):
    size = K * CL
    loads, saves = [], []
    for f in range(F):
        cut = pl.ds(f * size, size)
        loads.append(pltpu.make_async_copy(part.at[cut], held.at[cut], sems.at[f]))
        saves.append(pltpu.make_async_copy(held.at[cut], adjoint.at[cut], sems.at[F + f]))
        loads[f].start()

    flat = jnp.transpose(returned[pl.ds(0, NDEV, stride=MESSAGE), :])[:CAP]
    flat = jnp.concatenate(thirds(flat), axis=0)
    dest = iota((NDEV, 128), 0)
    place = iota((CAP, 128), 0).astype(f32)
    for b in range(NBLK):
        hot = (dest == owner[b : b + 1, :]).astype(f32).astype(jnp.bfloat16)
        found = jnp.dot(flat, hot, preferred_element_type=f32)
        found = found[:CAP] + found[CAP : 2 * CAP] + found[2 * CAP :]
        departures[b : b + 1, :] = jnp.sum(
            jnp.where(place == slots[b : b + 1, :], found, 0.0), axis=0, keepdims=True
        )

    odd, top, bottom = where_am_i()
    lane = iota((CL, CW), 1)
    slot = lane & 3
    close = (lane < 2) | (lane >= CW - 2)
    for f in range(F):
        merged = jnp.where(slot < 2, from_east[f], from_west[f])
        loads[f].wait()

        @pl.loop(0, K, unroll=K)
        def _(level):
            more = pltpu.roll(merged, 126 - 4 * level, axis=1)
            at = pl.multiple_of((f * K + level) * CL, CL)
            held[pl.ds(at, CL), :] = held[pl.ds(at, CL), :] + jnp.where(close, more, 0.0)

        north_line = corner_line(returned, f, NE, NW)
        north_line = jnp.where(top, -north_line, north_line) if f in FLIPPED else north_line
        south_line = jnp.where(bottom, 0.0, corner_line(returned, f, SE, SW))
        for d in range(2):
            cut = slice(d * PLANES + f * K, d * PLANES + f * K + K)
            more_up = jnp.where(odd, got2[cut, :], got1[cut, :])
            more_down = jnp.where(odd, got1[cut, :], got2[cut, :])
            if d == 0:
                more_up = more_up + jnp.where(close, spread(north_line), 0.0)
                more_down = more_down + jnp.where(close, spread(south_line), 0.0)
            up = pl.ds(f * size + CL - 1 - d, K, stride=CL)
            held[up, :] = held[up, :] + more_up
            down = pl.ds(f * size + d, K, stride=CL)
            held[down, :] = held[down, :] + more_down
        saves[f].start()
    for copy in saves:
        copy.wait()


def all_to_all(x):
    shape = x.shape
    x = x.reshape(NDEV, 1, MESSAGE * CW)
    x = lax.all_to_all(x, ("lon", "lat"), split_axis=0, concat_axis=0, tiled=True)
    return x.reshape(shape)


def shards(
    background, velocity, diffusivity, obs_value, obs_weight, obs_owner, obs_counts, obs_cell
):
    nlon = lax.axis_size("lon")
    nlat = lax.axis_size("lat")
    both = ("lon", "lat")

    def number(i, j):
        return i * nlat + j

    pairs1 = [(number(i, j), number(i, j ^ 1)) for i in range(nlon) for j in range(nlat)]
    pairs2 = []
    for i in range(nlon):
        for j in range(1, nlat - 1):
            pairs2.append((number(i, j), number(i, j + 1 if j & 1 else j - 1)))
        pairs2.append((number(i, nlat - 1), number(nlon - 1 - i, nlat - 1)))
    eastward = [(i, (i + 1) % nlon) for i in range(nlon)]
    westward = [((i + 1) % nlon, i) for i in range(nlon)]

    def around(x):
        return lax.ppermute(x, "lon", eastward), lax.ppermute(x, "lon", westward)

    x = background.reshape(ROWS, CW)
    vel = velocity.reshape(2 * K * CL, CW)
    own, pay1, pay2 = call(
        edges_kernel,
        [((F + 2, CL, CW), f32)] + [((ALL + PLANES, CW), f32)] * 2,
        [(H, x), (H, vel)],
        "edges",
        scratch=[V((ALL * CL, CW), f32), pltpu.SemaphoreType.DMA((F + 2,))],
    )
    got2 = lax.ppermute(pay2, both, pairs2)
    got1 = lax.ppermute(pay1, both, pairs1)
    from_west, from_east = around(own)

    owner = obs_owner.reshape(NBLK, 128)
    packed, slots = call(
        pack_kernel,
        [((MESSAGE * NDEV, CW), f32), ((NBLK, 128), f32)],
        [
            (S, obs_counts),
            (V, obs_value.reshape(NBLK, 128)),
            (V, obs_weight.reshape(NBLK, 128)),
            (V, owner),
            (V, obs_cell.reshape(NBLK, 128)),
            (V, own),
        ],
        "pack",
    )
    arrived = all_to_all(packed)
    padded = 3 * ROWS + 2 * PAD
    replies, forecast, part, pay1, pay2, spill = call(
        core_kernel,
        [
            ((MESSAGE * NDEV, CW), f32),
            ((ROWS, CW), f32, H),
            ((ROWS, CW), f32, H),
            ((2 * PLANES, CW), f32),
            ((2 * PLANES, CW), f32),
            ((F, CL, CW), f32),
        ],
        [
            (S, diffusivity),
            (V, arrived),
            (H, x),
            (H, vel),
            (V, got1),
            (V, got2),
            (V, own),
            (V, from_west),
            (V, from_east),
        ],
        "core",
        scratch=[
            V((padded, CW), f32),
            V((padded, CW), f32),
            V((2 * K * CL + 2 * PAD, CW), f32),
            V((CAP * NDEV, CW), f32),
            V((CAP * NDEV, CW), f32),
            V((CAP * NDEV, CW), i32),
            V((CAP, 128), i32),
            S((CAP, 128), i32),
            V((4, ALL, CW), f32),
            V((2, PLANES, CW), f32),
            V((F + 2, EXT, CW), f32),
            V((F + 2, EXT, CW), f32),
            V((F, EXT, CW), f32),
            V((F, EXT, CW), f32),
            V((F, EXT, CW), f32),
            V((F, EXT, CW), f32),
            pltpu.SemaphoreType.DMA((4 + 2 * F,)),
        ],
    )
    back2 = lax.ppermute(pay2, both, pairs2)
    back1 = lax.ppermute(pay1, both, pairs1)
    spill_west, spill_east = around(spill)
    returned = all_to_all(replies)
    adjoint, found = call(
        finish_kernel,
        [((ROWS, CW), f32, H), ((NBLK, 128), f32)],
        [
            (H, part),
            (V, spill_west),
            (V, spill_east),
            (V, back1),
            (V, back2),
            (V, returned),
            (V, owner),
            (V, slots),
        ],
        "finish",
        scratch=[V((ROWS, CW), f32), pltpu.SemaphoreType.DMA((2 * F,))],
    )
    shape = (F, K, CL, CW)
    return forecast.reshape(shape), adjoint.reshape(shape), found.reshape(-1)


def solution(mesh):
    in_specs = (
        P(None, None, "lat", "lon"),
        P(None, None, "lat", "lon"),
        P(),
        P(("lon", "lat")),
        P(("lon", "lat")),
        P(("lon", "lat"), None),
        P(("lon", "lat"), None),
        P(("lon", "lat")),
    )
    out_specs = (P(None, None, "lat", "lon"), P(None, None, "lat", "lon"), P(("lon", "lat")))
    return jax.shard_map(shards, mesh=mesh, in_specs=in_specs, out_specs=out_specs, check_vma=False)
```

profile of v0, /device:TPU:62, one launch (start us, length us, event | category | flops | bytes accessed | tf_op | source)
XLA Modules:
  0.0 84.9 jit_solution(7714831723270763852)
XLA Ops:
  0.6 0.0 copy-start.3
  0.6 0.0 copy-start.4
  0.7 0.0 copy-start
  0.7 0.0 copy-start.2
  0.7 2.8 %edges.1 = (f32[7,32,128]{2,1,0:T(8,128)S(1)}, f32[384,128]{1,0:T(8,128)S(1)}, f32[384,128]{1,0:T(8,128)S(1)}) custom-call(f32[5120,128]{1,0:T(8,128)} %bitcast.19, f32[2048,128]{1,0:T(8,128)} %bitcast.21), custom_call_target="tpu_custom_call" | custom-call | flops 1000000 | bytes 1000000 | tf_op jit(solution)/shard_map/edges/pallas_call | solution.py:36
  3.5 0.8 collective-permute-start
  4.3 5.4 %collective-permute-start.1 = (f32[384,128]{1,0:T(8,128)S(1)}, f32[384,128]{1,0:T(8,128)S(1)}, u32[]{:S(2)}, u32[]{:S(2)}) collective-permute-start(f32[384,128]{1,0:T(8,128)S(1)} %get-tuple-element.19), channel_id=1, source_target_pairs={{1,2},{2,1},{3,4},{4,3},{5,6},{6,5},{7,127},{9,10},{10,9},{11,12},... | collective-permute-start | bytes 589832 | tf_op jit(solution)/shard_map/ppermute | solution.py:689
  9.7 2.9 %pack.1 = (f32[384,128]{1,0:T(8,128)}, f32[8,128]{1,0:T(8,128)S(1)}) custom-call(s32[1,8]{1,0:T(1,128)S(1)} %copy-done.4, f32[8,128]{1,0:T(8,128)S(1)} %bitcast.16, f32[8,128]{1,0:T(8,128)S(1)} %bitcast.17, s32[8,128]{1,0:T(8,128)S(1)} %bitcast.14, s32[8,128]{1,0:T(8,128)S(1)} %bitcast.18, f32[7,32,128]{2,1,0:T(8,128)S(1)} %get-tuple-element.16.own), custom_call_target="tpu_custom_call" | custom-call | flops 1000000 | bytes 1000000 | tf_op jit(solution)/shard_map/pack/pallas_call | solution.py:36
  12.6 7.8 %all-to-all-start = ((f32[128,1,384]{2,1,0:T(1,128)}), f32[128,1,384]{2,1,0:T(1,128)S(1)}, u32[]{:S(2)}, u32[]{:S(2)}) async-start(f32[128,1,384]{2,1,0:T(1,128)} %bitcast.6), calls=%async_computation | async-start | bytes 393216 | tf_op jit(solution)/shard_map/all_to_all | solution.py:654
  20.4 0.1 collective-permute-start.3
  20.5 0.5 collective-permute-start.2
  21.0 2.9 %collective-permute-done.3.from_east = f32[7,32,128]{2,1,0:T(8,128)S(1)} collective-permute-done((f32[7,32,128]{2,1,0:T(8,128)S(1)}, f32[7,32,128]{2,1,0:T(8,128)S(1)}, u32[]{:S(2)}, u32[]{:S(2)}) %collective-permute-start.3) | collective-permute-done | bytes 114720 | tf_op jit(solution)/shard_map/ppermute | solution.py:678
  23.9 1.1 %collective-permute-done.2.from_west = f32[7,32,128]{2,1,0:T(8,128)S(1)} collective-permute-done((f32[7,32,128]{2,1,0:T(8,128)S(1)}, f32[7,32,128]{2,1,0:T(8,128)S(1)}, u32[]{:S(2)}, u32[]{:S(2)}) %collective-permute-start.2) | collective-permute-done | bytes 114720 | tf_op jit(solution)/shard_map/ppermute | solution.py:678
  25.0 1.7 %all-to-all-done = f32[128,1,384]{2,1,0:T(1,128)S(1)} async-done(((f32[128,1,384]{2,1,0:T(1,128)}), f32[128,1,384]{2,1,0:T(1,128)S(1)}, u32[]{:S(2)}, u32[]{:S(2)}) %all-to-all-start) | async-done | bytes 196640 | tf_op jit(solution)/shard_map/all_to_all | solution.py:654
  26.6 0.0 collective-permute-done.got1
  26.7 0.0 collective-permute-done.1.got2
  26.7 0.0 copy-start.8
  26.7 0.7 copy-done.6
  27.3 0.1 copy-done.7
  27.4 0.0 copy-done.8
  27.4 26.0 %core.1 = (f32[384,128]{1,0:T(8,128)}, f32[5120,128]{1,0:T(8,128)}, f32[5120,128]{1,0:T(8,128)}, f32[320,128]{1,0:T(8,128)S(1)}, f32[320,128]{1,0:T(8,128)S(1)}, /*index=5*/f32[5,32,128]{2,1,0:T(8,128)S(1)}) custom-call(f32[5]{0:T(128)S(1)} %copy-done.5, f32[384,128]{1,0:T(8,128)} %bitcast.23, f32[5120,128]{1,0:T(8,128)} %bitcast.20, f32[2048,128]{1,0:T(8,128)} %bitcast.22, ...), custom_call_target="tpu_custom_call" | custom-call | flops 1000000 | bytes 1000000 | tf_op jit(solution)/shard_map/core/pallas_call | solution.py:36
  53.5 10.8 %all-to-all-start.1 = ((f32[128,1,384]{2,1,0:T(1,128)}), f32[128,1,384]{2,1,0:T(1,128)S(1)}, u32[]{:S(2)}, u32[]{:S(2)}) async-start(f32[128,1,384]{2,1,0:T(1,128)} %bitcast.9), calls=%async_computation.1 | async-start | bytes 393216 | tf_op jit(solution)/shard_map/all_to_all | solution.py:654
  64.3 0.9 %collective-permute-start.6 = (f32[320,128]{1,0:T(8,128)S(1)}, f32[320,128]{1,0:T(8,128)S(1)}, u32[]{:S(2)}, u32[]{:S(2)}) collective-permute-start(f32[320,128]{1,0:T(8,128)S(1)} %get-tuple-element.23), channel_id=1, source_target_pairs={{0,1},{1,0},{2,3},{3,2},{4,5},{5,4},{6,7},{7,6},{8,9},{9,8},{10,11... | collective-permute-start | bytes 491528 | tf_op jit(solution)/shard_map/ppermute | solution.py:752
  65.2 5.0 %collective-permute-start.7 = (f32[320,128]{1,0:T(8,128)S(1)}, f32[320,128]{1,0:T(8,128)S(1)}, u32[]{:S(2)}, u32[]{:S(2)}) collective-permute-start(f32[320,128]{1,0:T(8,128)S(1)} %get-tuple-element.24), channel_id=1, source_target_pairs={{1,2},{2,1},{3,4},{4,3},{5,6},{6,5},{7,127},{9,10},{10,9},{11,12},... | collective-permute-start | bytes 491528 | tf_op jit(solution)/shard_map/ppermute | solution.py:751
  70.2 0.5 collective-permute-start.5
  70.7 0.1 collective-permute-start.4
  70.8 1.9 %collective-permute-done.5.from_east = f32[5,32,128]{2,1,0:T(8,128)S(1)} collective-permute-done((f32[5,32,128]{2,1,0:T(8,128)S(1)}, f32[5,32,128]{2,1,0:T(8,128)S(1)}, u32[]{:S(2)}, u32[]{:S(2)}) %collective-permute-start.5) | collective-permute-done | bytes 81952 | tf_op jit(solution)/shard_map/ppermute | solution.py:678
  72.7 1.8 %collective-permute-done.4.from_west = f32[5,32,128]{2,1,0:T(8,128)S(1)} collective-permute-done((f32[5,32,128]{2,1,0:T(8,128)S(1)}, f32[5,32,128]{2,1,0:T(8,128)S(1)}, u32[]{:S(2)}, u32[]{:S(2)}) %collective-permute-start.4) | collective-permute-done | bytes 81952 | tf_op jit(solution)/shard_map/ppermute | solution.py:678
  74.5 0.0 collective-permute-done.6.got1
  74.5 6.4 %collective-permute-done.7.got2 = f32[320,128]{1,0:T(8,128)S(1)} collective-permute-done((f32[320,128]{1,0:T(8,128)S(1)}, f32[320,128]{1,0:T(8,128)S(1)}, u32[]{:S(2)}, u32[]{:S(2)}) %collective-permute-start.7) | collective-permute-done | bytes 163872 | tf_op jit(solution)/shard_map/ppermute | solution.py:751
  80.9 0.0 all-to-all-done.1
  80.9 4.0 %finish.1 = (f32[5120,128]{1,0:T(8,128)}, f32[8,128]{1,0:T(8,128)}) custom-call(f32[5120,128]{1,0:T(8,128)} %get-tuple-element.21.part, f32[5,32,128]{2,1,0:T(8,128)S(1)} %collective-permute-done.4.from_west, f32[5,32,128]{2,1,0:T(8,128)S(1)} %collective-permute-done.5.from_east, f32[320,128]{1,0:T(8,128)S(1)} %collective-permute-done.6.got1, ...), custom_call_target="tpu_custom_call" | custom-call | flops 1000000 | bytes 1000000 | tf_op jit(solution)/shard_map/finish/pallas_call | solution.py:36
  (10 shorter events, 0.0 us)
Async XLA Ops:
  0.6 9.0 %copy-start.3 = (s32[1024]{0:T(1024)S(1)}, s32[1024]{0:T(1024)}, u32[]{:S(2)}) copy-start(s32[1024]{0:T(1024)} %param.15) | copy-start | bytes 12292
  0.6 9.0 %copy-start.4 = (s32[1,8]{1,0:T(1,128)S(1)}, s32[1,8]{1,0:T(1,128)}, u32[]{:S(2)}) copy-start(s32[1,8]{1,0:T(1,128)} %counts.1) | copy-start | bytes 100
  0.7 9.0 %copy-start = (s32[1024,1]{0,1:T(1,128)S(1)}, s32[1024,1]{0,1:T(1,128)}, u32[]{:S(2)}) copy-start(s32[1024,1]{0,1:T(1,128)} %param.13) | copy-start | bytes 12292
  0.7 9.0 %copy-start.2 = (f32[1024]{0:T(1024)S(1)}, f32[1024]{0:T(1024)}, u32[]{:S(2)}) copy-start(f32[1024]{0:T(1024)} %param.12) | copy-start | bytes 12292
  0.7 9.0 %copy-start.1 = (f32[1024]{0:T(1024)S(1)}, f32[1024]{0:T(1024)}, u32[]{:S(2)}) copy-start(f32[1024]{0:T(1024)} %param.11) | copy-start | bytes 12292
  0.7 26.8 %copy-start.5 = (f32[5]{0:T(128)S(1)}, f32[5]{0:T(128)}, u32[]{:S(2)}) copy-start(f32[5]{0:T(128)} %kap.1) | copy-start | bytes 64
  3.5 23.2 %collective-permute-start = (f32[384,128]{1,0:T(8,128)S(1)}, f32[384,128]{1,0:T(8,128)S(1)}, u32[]{:S(2)}, u32[]{:S(2)}) collective-permute-start(f32[384,128]{1,0:T(8,128)S(1)} %get-tuple-element.18), channel_id=1, source_target_pairs={{0,1},{1,0},{2,3},{3,2},{4,5},{5,4},{6,7},{7,6},{8,9},{9,8},{10,11... | collective-permute-start | bytes 589832 | tf_op jit(solution)/shard_map/ppermute | solution.py:690
  4.3 22.4 %collective-permute-start.1 = (f32[384,128]{1,0:T(8,128)S(1)}, f32[384,128]{1,0:T(8,128)S(1)}, u32[]{:S(2)}, u32[]{:S(2)}) collective-permute-start(f32[384,128]{1,0:T(8,128)S(1)} %get-tuple-element.19), channel_id=1, source_target_pairs={{1,2},{2,1},{3,4},{4,3},{5,6},{6,5},{7,127},{9,10},{10,9},{11,12},... | collective-permute-start | bytes 589832 | tf_op jit(solution)/shard_map/ppermute | solution.py:689
  12.6 14.0 %all-to-all-start = ((f32[128,1,384]{2,1,0:T(1,128)}), f32[128,1,384]{2,1,0:T(1,128)S(1)}, u32[]{:S(2)}, u32[]{:S(2)}) async-start(f32[128,1,384]{2,1,0:T(1,128)} %bitcast.6), calls=%async_computation | async-start | bytes 393216 | tf_op jit(solution)/shard_map/all_to_all | solution.py:654
  20.4 3.5 %collective-permute-start.3 = (f32[7,32,128]{2,1,0:T(8,128)S(1)}, f32[7,32,128]{2,1,0:T(8,128)S(1)}, u32[]{:S(2)}, u32[]{:S(2)}) collective-permute-start(f32[7,32,128]{2,1,0:T(8,128)S(1)} %get-tuple-element.16.own), channel_id=1, source_target_pairs={{8,0},{16,8},{24,16},{32,24},{40,32},{48,40},{56,48},{64,56},{72,6... | collective-permute-start | bytes 344072 | tf_op jit(solution)/shard_map/ppermute | solution.py:678
  20.5 4.5 %collective-permute-start.2 = (f32[7,32,128]{2,1,0:T(8,128)S(1)}, f32[7,32,128]{2,1,0:T(8,128)S(1)}, u32[]{:S(2)}, u32[]{:S(2)}) collective-permute-start(f32[7,32,128]{2,1,0:T(8,128)S(1)} %get-tuple-element.16.own), channel_id=1, source_target_pairs={{0,8},{8,16},{16,24},{24,32},{32,40},{40,48},{48,56},{56,64},{64,7... | collective-permute-start | bytes 344072 | tf_op jit(solution)/shard_map/ppermute | solution.py:678
  26.6 0.7 copy-start.6
  26.6 0.8 copy-start.7
  26.7 0.8 copy-start.8
  53.5 27.5 %all-to-all-start.1 = ((f32[128,1,384]{2,1,0:T(1,128)}), f32[128,1,384]{2,1,0:T(1,128)S(1)}, u32[]{:S(2)}, u32[]{:S(2)}) async-start(f32[128,1,384]{2,1,0:T(1,128)} %bitcast.9), calls=%async_computation.1 | async-start | bytes 393216 | tf_op jit(solution)/shard_map/all_to_all | solution.py:654
  64.3 10.2 %collective-permute-start.6 = (f32[320,128]{1,0:T(8,128)S(1)}, f32[320,128]{1,0:T(8,128)S(1)}, u32[]{:S(2)}, u32[]{:S(2)}) collective-permute-start(f32[320,128]{1,0:T(8,128)S(1)} %get-tuple-element.23), channel_id=1, source_target_pairs={{0,1},{1,0},{2,3},{3,2},{4,5},{5,4},{6,7},{7,6},{8,9},{9,8},{10,11... | collective-permute-start | bytes 491528 | tf_op jit(solution)/shard_map/ppermute | solution.py:752
  65.2 15.8 %collective-permute-start.7 = (f32[320,128]{1,0:T(8,128)S(1)}, f32[320,128]{1,0:T(8,128)S(1)}, u32[]{:S(2)}, u32[]{:S(2)}) collective-permute-start(f32[320,128]{1,0:T(8,128)S(1)} %get-tuple-element.24), channel_id=1, source_target_pairs={{1,2},{2,1},{3,4},{4,3},{5,6},{6,5},{7,127},{9,10},{10,9},{11,12},... | collective-permute-start | bytes 491528 | tf_op jit(solution)/shard_map/ppermute | solution.py:751
  70.2 2.5 %collective-permute-start.5 = (f32[5,32,128]{2,1,0:T(8,128)S(1)}, f32[5,32,128]{2,1,0:T(8,128)S(1)}, u32[]{:S(2)}, u32[]{:S(2)}) collective-permute-start(f32[5,32,128]{2,1,0:T(8,128)S(1)} %get-tuple-element.22), channel_id=1, source_target_pairs={{8,0},{16,8},{24,16},{32,24},{40,32},{48,40},{56,48},{64,56},{72,6... | collective-permute-start | bytes 245768 | tf_op jit(solution)/shard_map/ppermute | solution.py:678
  70.7 3.9 %collective-permute-start.4 = (f32[5,32,128]{2,1,0:T(8,128)S(1)}, f32[5,32,128]{2,1,0:T(8,128)S(1)}, u32[]{:S(2)}, u32[]{:S(2)}) collective-permute-start(f32[5,32,128]{2,1,0:T(8,128)S(1)} %get-tuple-element.22), channel_id=1, source_target_pairs={{0,8},{8,16},{16,24},{24,32},{32,40},{40,48},{48,56},{56,64},{64,7... | collective-permute-start | bytes 245768 | tf_op jit(solution)/shard_map/ppermute | solution.py:678
where the time goes:
time: 85.2 us; the launch traced here: 84.9 us
  Pallas kernels  35.6 us (42%)
  starting transfers between devices  31.8 us (37%)
  waiting for transfers between devices  15.8 us (19%)
    pallas_call x4, Pallas kernels, call(): pl.pallas_call(body, out_shape=[jax.ShapeDtypeStruct(shape, dtype) for sh...  35.6 us
    all_to_all x2, starting transfers between devices, all_to_all(): lax.all_to_all(x, ('lon', 'lat'), split_axis=0, concat_axis=0, tiled=True)  18.6 us
    ppermute x4, waiting for transfers between devices, around(): return (lax.ppermute(x, 'lon', eastward), lax.ppermute(x, 'lon', westward))  7.74 us
    ppermute x1, waiting for transfers between devices, shards(): back2 = lax.ppermute(pay2, both, pairs2)  6.39 us
    ppermute x1, starting transfers between devices, shards(): got2 = lax.ppermute(pay2, both, pairs2)  5.37 us
    ppermute x1, starting transfers between devices, shards(): back2 = lax.ppermute(pay2, both, pairs2)  5.04 us
  transfers between devices with their start and end apart: 10, of which 6 were waited for; matrix products, arithmetic and copies ran while one was open for 0% of the time, Pallas kernels for 3%

commit v1 on v0

--- a/solution.py
+++ b/solution.py
@@ -74,38 +74,44 @@
 
 
 def corner_rows(blocks, line, place):
-    slot = iota((8, CW), 1) & 3
-    rows = []
-    for start in range(0, len(blocks), 4):
-        row = jnp.zeros((8, CW), f32)
-        for kind, block in enumerate(blocks[start : start + 4]):
-            row = jnp.where(slot == kind, pltpu.roll(block, (kind - place) % CW, axis=1), row)
-        rows.append(row[line : line + 1])
-    return rows
+    lane = iota((8, CW), 1)
+    row = jnp.zeros((8, CW), f32)
+    for f in range(F - 1):
+        row = jnp.where(lane & 3 == f, pltpu.roll(blocks[f], (f - place) % CW, axis=1), row)
+    picked = (4 * (lane - TAIL) + place) & (CW - 1)
+    tail = jnp.take_along_axis(blocks[F - 1], picked, axis=1)
+    return tail[line : line + 1], row[line : line + 1]
 
 
 def post_corners(pay, rows, bottom):
+    tail = iota((1, CW), 1) >= TAIL
     for n, at in enumerate(partners()):
-        for r in range(2):
-            @pl.when(jnp.logical_not(bottom) if n >= 2 else at >= 0)
-            def _(n=n, at=at, r=r):
-                pay[pl.ds(MESSAGE * at + 1 + r, 1), :] = rows[n][r]
-
-
-def corner_line(got, kind, first, second):
-    slot = iota((8, CW), 1) & 3
+        @pl.when(jnp.logical_not(bottom) if n >= 2 else at >= 0)
+        def _(n=n, at=at):
+            to = pl.ds(MESSAGE * at, 1)
+            pay[to, :] = jnp.where(tail, rows[n][0], pay[to, :])
+            pay[pl.ds(MESSAGE * at + 1, 1), :] = rows[n][1]
+
+
+def corner_line(got, f, first, second):
+    lane = iota((8, CW), 1)
     ats = partners()
     line = jnp.zeros((8, CW), f32)
     for place, n in ((1, first), (2, second)):
-        row = got[pl.ds(MESSAGE * ats[n] + 1 + kind // 4, 1), :]
-        moved = pltpu.roll(jnp.broadcast_to(row, (8, CW)), (place - kind % 4) % CW, axis=1)
-        line = jnp.where(slot == place, moved, line)
+        row = got[pl.ds(MESSAGE * ats[n] + (0 if f == F - 1 else 1), 1), :]
+        row = jnp.broadcast_to(row, (8, CW))
+        if f == F - 1:
+            moved = jnp.take_along_axis(row, TAIL + (lane >> 2), axis=1)
+        else:
+            moved = pltpu.roll(row, (place - f) % CW, axis=1)
+        line = jnp.where(lane & 3 == place, moved, line)
     return line[:1]
 
 
 NE, NW, SE, SW = range(4)
-MESSAGE = 3
-FLIPPED = (2, 3, 5, 6)
+MESSAGE = 2
+TAIL = CW - K
+FLIPPED = (2, 3)
 
 
 def thirds(x):
@@ -236,8 +242,8 @@
         )
     pay[...] = jnp.zeros(pay.shape, f32)
     pay[pl.ds(0, NDEV, stride=MESSAGE), :] = total
-    low = [own[kind, :8, :] for kind in range(F + 2)]
-    high = [own[kind, CL - 8 :, :] for kind in range(F + 2)]
+    low = [own[f, :8, :] for f in range(F)]
+    high = [own[f, CL - 8 :, :] for f in range(F)]
     _, _, bottom = where_am_i()
     post_corners(
         pay,
@@ -253,7 +259,7 @@
 
 PAD = 8
 GROUP = 8
-UNROLL = 4
+UNROLL = 8
 TILES = CL // 8
 
 
@@ -284,10 +290,11 @@
         span = slice(kind * K, kind * K + K)
         mine_all[kind, CL : CL + 1, :] = gather_line(halo[0, span, :])
         mine_all[kind, EXT - 1 :, :] = gather_line(halo[2, span, :])
-        line = corner_line(arrived, kind, NW, NE)
-        side[kind, CL : CL + 1, :] = jnp.where(top, -line, line) if kind in FLIPPED else line
-        line = corner_line(arrived, kind, SW, SE)
-        side[kind, EXT - 1 :, :] = jnp.where(bottom, 0.0, line)
+        if kind < F:
+            line = corner_line(arrived, kind, NW, NE)
+            side[kind, CL : CL + 1, :] = jnp.where(top, -line, line) if kind in FLIPPED else line
+            line = corner_line(arrived, kind, SW, SE)
+            side[kind, EXT - 1 :, :] = jnp.where(bottom, 0.0, line)
     base, um, up, vm, vp = parts(side[F], side[F + 1])
     for f in range(F):
         k = kap[f]
@@ -394,7 +401,7 @@
 
     load_i.wait()
 
-    @pl.loop(0, NDEV)
+    @pl.loop(0, NDEV, unroll=4)
     def _(s):
         for q in range(CAP):
             at = index_s[q, s]
@@ -431,7 +438,7 @@
                 acc = acc + jnp.where(mine == cell_of[other, :] >> 7, adds[other, :], 0.0)
             adds[cut, :] = acc
 
-    @pl.loop(0, NDEV)
+    @pl.loop(0, NDEV, unroll=4)
     def _(s):
         for start in range(0, CAP, GROUP):
             ats = [index_s[q, s] for q in range(start, start + GROUP)]
@@ -687,7 +694,6 @@
         scratch=[V((ALL * CL, CW), f32), pltpu.SemaphoreType.DMA((F + 2,))],
     )
     got2 = lax.ppermute(pay2, both, pairs2)
-    got1 = lax.ppermute(pay1, both, pairs1)
     from_west, from_east = around(own)
 
     owner = obs_owner.reshape(NBLK, 128)
@@ -704,6 +710,8 @@
         ],
         "pack",
     )
+    pay1, packed = lax.optimization_barrier((pay1, packed))
+    got1 = lax.ppermute(pay1, both, pairs1)
     arrived = all_to_all(packed)
     padded = 3 * ROWS + 2 * PAD
     replies, forecast, part, pay1, pay2, spill = call(

time: 85.2 us -> 82.7 us (0.971)
  the two profiles are of different devices: /device:TPU:62 before, /device:TPU:1 now
where the time goes in v1:
time: 82.7 us; the launch traced here: 82.4 us
  Pallas kernels  33.6 us (41%)
  starting transfers between devices  31.2 us (38%)
  waiting for transfers between devices  16.1 us (19%)
    pallas_call x4, Pallas kernels, call(): pl.pallas_call(body, out_shape=[jax.ShapeDtypeStruct(shape, dtype) for sh...  33.6 us
    all_to_all x2, starting transfers between devices, all_to_all(): lax.all_to_all(x, ('lon', 'lat'), split_axis=0, concat_axis=0, tiled=True)  23.5 us
    all_to_all x2, waiting for transfers between devices, all_to_all(): lax.all_to_all(x, ('lon', 'lat'), split_axis=0, concat_axis=0, tiled=True)  9.13 us
    ppermute x4, waiting for transfers between devices, around(): return (lax.ppermute(x, 'lon', eastward), lax.ppermute(x, 'lon', westward))  6.91 us
    ppermute x4, starting transfers between devices, around(): return (lax.ppermute(x, 'lon', eastward), lax.ppermute(x, 'lon', westward))  3.81 us
    ppermute x1, starting transfers between devices, shards(): got1 = lax.ppermute(pay1, both, pairs1)  2.12 us
  transfers between devices with their start and end apart: 10, of which 6 were waited for; matrix products, arithmetic and copies ran while one was open for 0% of the time, Pallas kernels for 0%

profile of v1, /device:TPU:1, one launch (start us, length us, event | category | flops | bytes accessed | tf_op | source)
XLA Modules:
  0.0 82.4 jit_solution(1854327326933295334)
XLA Ops:
  0.6 0.0 copy-start.3
  0.6 0.0 copy-start.4
  0.7 0.0 copy-start
  0.7 0.0 copy-start.2
  0.7 0.0 copy-start.1
  0.7 0.0 copy-start.5
  0.7 2.8 %edges.1 = (f32[7,32,128]{2,1,0:T(8,128)S(1)}, f32[384,128]{1,0:T(8,128)S(1)}, f32[384,128]{1,0:T(8,128)S(1)}) custom-call(f32[5120,128]{1,0:T(8,128)} %bitcast.20, f32[2048,128]{1,0:T(8,128)} %bitcast.22), custom_call_target="tpu_custom_call" | custom-call | flops 1000000 | bytes 1000000 | tf_op jit(solution)/shard_map/edges/pallas_call | solution.py:36
  3.5 2.9 %pack.1 = (f32[256,128]{1,0:T(8,128)}, f32[8,128]{1,0:T(8,128)S(1)}) custom-call(s32[1,8]{1,0:T(1,128)S(1)} %copy-done.4, f32[8,128]{1,0:T(8,128)S(1)} %bitcast.17, f32[8,128]{1,0:T(8,128)S(1)} %bitcast.18, s32[8,128]{1,0:T(8,128)S(1)} %bitcast.15, s32[8,128]{1,0:T(8,128)S(1)} %bitcast.19, f32[7,32,128]{2,1,0:T(8,128)S(1)} %get-tuple-element.19.own), custom_call_target="tpu_custom_call" | custom-call | flops 1000000 | bytes 1000000 | tf_op jit(solution)/shard_map/pack/pallas_call | solution.py:36
  6.4 2.1 %collective-permute-start = (f32[384,128]{1,0:T(8,128)S(1)}, f32[384,128]{1,0:T(8,128)S(1)}, u32[]{:S(2)}, u32[]{:S(2)}) collective-permute-start(f32[384,128]{1,0:T(8,128)S(1)} %get-tuple-element.22), channel_id=1, source_target_pairs={{0,1},{1,0},{2,3},{3,2},{4,5},{5,4},{6,7},{7,6},{8,9},{9,8},{10,11... | collective-permute-start | bytes 589832 | tf_op jit(solution)/shard_map/ppermute | solution.py:714
  8.6 0.7 collective-permute-start.1
  9.2 12.5 %all-to-all-start = ((f32[128,1,256]{2,1,0:T(1,128)}), f32[128,1,256]{2,1,0:T(1,128)S(1)}, u32[]{:S(2)}, u32[]{:S(2)}) async-start(f32[128,1,256]{2,1,0:T(1,128)} %bitcast.6), calls=%async_computation | async-start | bytes 262144 | tf_op jit(solution)/shard_map/all_to_all | solution.py:661
  21.8 1.1 %collective-permute-start.3 = (f32[7,32,128]{2,1,0:T(8,128)S(1)}, f32[7,32,128]{2,1,0:T(8,128)S(1)}, u32[]{:S(2)}, u32[]{:S(2)}) collective-permute-start(f32[7,32,128]{2,1,0:T(8,128)S(1)} %get-tuple-element.19.own), channel_id=1, source_target_pairs={{8,0},{16,8},{24,16},{32,24},{40,32},{48,40},{56,48},{64,56},{72,6... | collective-permute-start | bytes 344072 | tf_op jit(solution)/shard_map/ppermute | solution.py:685
  22.9 0.8 collective-permute-start.2
  23.7 3.2 %collective-permute-done.3.from_east = f32[7,32,128]{2,1,0:T(8,128)S(1)} collective-permute-done((f32[7,32,128]{2,1,0:T(8,128)S(1)}, f32[7,32,128]{2,1,0:T(8,128)S(1)}, u32[]{:S(2)}, u32[]{:S(2)}) %collective-permute-start.3) | collective-permute-done | bytes 114720 | tf_op jit(solution)/shard_map/ppermute | solution.py:685
  26.8 0.8 collective-permute-done.2.from_west
  27.6 4.1 %all-to-all-done = f32[128,1,256]{2,1,0:T(1,128)S(1)} async-done(((f32[128,1,256]{2,1,0:T(1,128)}), f32[128,1,256]{2,1,0:T(1,128)S(1)}, u32[]{:S(2)}, u32[]{:S(2)}) %all-to-all-start) | async-done | bytes 131104 | tf_op jit(solution)/shard_map/all_to_all | solution.py:661
  31.7 0.0 collective-permute-done.got1
  31.7 0.0 collective-permute-done.1.got2
  31.7 0.7 copy-done.6
  32.4 0.1 copy-done.7
  32.4 23.9 %core.1 = (f32[256,128]{1,0:T(8,128)}, f32[5120,128]{1,0:T(8,128)}, f32[5120,128]{1,0:T(8,128)}, f32[320,128]{1,0:T(8,128)S(1)}, f32[320,128]{1,0:T(8,128)}, /*index=5*/f32[5,32,128]{2,1,0:T(8,128)S(1)}) custom-call(f32[5]{0:T(128)S(1)} %copy-done.5, f32[256,128]{1,0:T(8,128)S(1)} %bitcast.13, f32[5120,128]{1,0:T(8,128)} %bitcast.21, f32[2048,128]{1,0:T(8,128)} %bitcast.23, ...), custom_call_target="tpu_custom_call" | custom-call | flops 1000000 | bytes 1000000 | tf_op jit(solution)/shard_map/core/pallas_call | solution.py:36
  56.4 0.5 collective-permute-start.6
  56.8 0.7 collective-permute-start.7
  57.5 11.0 %all-to-all-start.1 = ((f32[128,1,256]{2,1,0:T(1,128)}), f32[128,1,256]{2,1,0:T(1,128)S(1)}, u32[]{:S(2)}, u32[]{:S(2)}) async-start(f32[128,1,256]{2,1,0:T(1,128)} %bitcast.9), calls=%async_computation.1 | async-start | bytes 262144 | tf_op jit(solution)/shard_map/all_to_all | solution.py:661
  68.5 1.1 %collective-permute-start.5 = (f32[5,32,128]{2,1,0:T(8,128)S(1)}, f32[5,32,128]{2,1,0:T(8,128)S(1)}, u32[]{:S(2)}, u32[]{:S(2)}) collective-permute-start(f32[5,32,128]{2,1,0:T(8,128)S(1)} %get-tuple-element.26), channel_id=1, source_target_pairs={{8,0},{16,8},{24,16},{32,24},{40,32},{48,40},{56,48},{64,56},{72,6... | collective-permute-start | bytes 245768 | tf_op jit(solution)/shard_map/ppermute | solution.py:685
  69.7 0.8 collective-permute-start.4
  70.4 2.7 %collective-permute-done.5.from_east = f32[5,32,128]{2,1,0:T(8,128)S(1)} collective-permute-done((f32[5,32,128]{2,1,0:T(8,128)S(1)}, f32[5,32,128]{2,1,0:T(8,128)S(1)}, u32[]{:S(2)}, u32[]{:S(2)}) %collective-permute-start.5) | collective-permute-done | bytes 81952 | tf_op jit(solution)/shard_map/ppermute | solution.py:685
  73.1 0.3 collective-permute-done.4.from_west
  73.4 5.0 %all-to-all-done.1 = f32[128,1,256]{2,1,0:T(1,128)S(1)} async-done(((f32[128,1,256]{2,1,0:T(1,128)}), f32[128,1,256]{2,1,0:T(1,128)S(1)}, u32[]{:S(2)}, u32[]{:S(2)}) %all-to-all-start.1) | async-done | bytes 131104 | tf_op jit(solution)/shard_map/all_to_all | solution.py:661
  78.4 0.0 collective-permute-done.6.got1
  78.4 0.0 collective-permute-done.7.got2
  78.5 4.0 %finish.1 = (f32[5120,128]{1,0:T(8,128)}, f32[8,128]{1,0:T(8,128)}) custom-call(f32[5120,128]{1,0:T(8,128)} %get-tuple-element.25.part, f32[5,32,128]{2,1,0:T(8,128)S(1)} %collective-permute-done.4.from_west, f32[5,32,128]{2,1,0:T(8,128)S(1)} %collective-permute-done.5.from_east, f32[320,128]{1,0:T(8,128)S(1)} %collective-permute-done.6.got1, ...), custom_call_target="tpu_custom_call" | custom-call | flops 1000000 | bytes 1000000 | tf_op jit(solution)/shard_map/finish/pallas_call | solution.py:36
  (8 shorter events, 0.0 us)
Async XLA Ops:
  0.6 2.8 %copy-start.3 = (s32[1024]{0:T(1024)S(1)}, s32[1024]{0:T(1024)}, u32[]{:S(2)}) copy-start(s32[1024]{0:T(1024)} %param.15) | copy-start | bytes 12292
  0.6 2.8 %copy-start.4 = (s32[1,8]{1,0:T(1,128)S(1)}, s32[1,8]{1,0:T(1,128)}, u32[]{:S(2)}) copy-start(s32[1,8]{1,0:T(1,128)} %counts.1) | copy-start | bytes 100
  0.7 2.8 %copy-start = (s32[1024,1]{0,1:T(1,128)S(1)}, s32[1024,1]{0,1:T(1,128)}, u32[]{:S(2)}) copy-start(s32[1024,1]{0,1:T(1,128)} %param.13) | copy-start | bytes 12292
  0.7 2.8 %copy-start.2 = (f32[1024]{0:T(1024)S(1)}, f32[1024]{0:T(1024)}, u32[]{:S(2)}) copy-start(f32[1024]{0:T(1024)} %param.12) | copy-start | bytes 12292
  0.7 2.8 %copy-start.1 = (f32[1024]{0:T(1024)S(1)}, f32[1024]{0:T(1024)}, u32[]{:S(2)}) copy-start(f32[1024]{0:T(1024)} %param.11) | copy-start | bytes 12292
  0.7 31.8 %copy-start.5 = (f32[5]{0:T(128)S(1)}, f32[5]{0:T(128)}, u32[]{:S(2)}) copy-start(f32[5]{0:T(128)} %kap.1) | copy-start | bytes 64
  6.4 25.3 %collective-permute-start = (f32[384,128]{1,0:T(8,128)S(1)}, f32[384,128]{1,0:T(8,128)S(1)}, u32[]{:S(2)}, u32[]{:S(2)}) collective-permute-start(f32[384,128]{1,0:T(8,128)S(1)} %get-tuple-element.22), channel_id=1, source_target_pairs={{0,1},{1,0},{2,3},{3,2},{4,5},{5,4},{6,7},{7,6},{8,9},{9,8},{10,11... | collective-permute-start | bytes 589832 | tf_op jit(solution)/shard_map/ppermute | solution.py:714
  8.6 23.1 %collective-permute-start.1 = (f32[384,128]{1,0:T(8,128)S(1)}, f32[384,128]{1,0:T(8,128)S(1)}, u32[]{:S(2)}, u32[]{:S(2)}) collective-permute-start(f32[384,128]{1,0:T(8,128)S(1)} %get-tuple-element.23), channel_id=1, source_target_pairs={{1,2},{2,1},{3,4},{4,3},{5,6},{6,5},{7,127},{9,10},{10,9},{11,12},... | collective-permute-start | bytes 589832 | tf_op jit(solution)/shard_map/ppermute | solution.py:696
  9.2 22.5 %all-to-all-start = ((f32[128,1,256]{2,1,0:T(1,128)}), f32[128,1,256]{2,1,0:T(1,128)S(1)}, u32[]{:S(2)}, u32[]{:S(2)}) async-start(f32[128,1,256]{2,1,0:T(1,128)} %bitcast.6), calls=%async_computation | async-start | bytes 262144 | tf_op jit(solution)/shard_map/all_to_all | solution.py:661
  21.8 5.1 %collective-permute-start.3 = (f32[7,32,128]{2,1,0:T(8,128)S(1)}, f32[7,32,128]{2,1,0:T(8,128)S(1)}, u32[]{:S(2)}, u32[]{:S(2)}) collective-permute-start(f32[7,32,128]{2,1,0:T(8,128)S(1)} %get-tuple-element.19.own), channel_id=1, source_target_pairs={{8,0},{16,8},{24,16},{32,24},{40,32},{48,40},{56,48},{64,56},{72,6... | collective-permute-start | bytes 344072 | tf_op jit(solution)/shard_map/ppermute | solution.py:685
  22.9 4.7 %collective-permute-start.2 = (f32[7,32,128]{2,1,0:T(8,128)S(1)}, f32[7,32,128]{2,1,0:T(8,128)S(1)}, u32[]{:S(2)}, u32[]{:S(2)}) collective-permute-start(f32[7,32,128]{2,1,0:T(8,128)S(1)} %get-tuple-element.19.own), channel_id=1, source_target_pairs={{0,8},{8,16},{16,24},{24,32},{32,40},{40,48},{48,56},{56,64},{64,7... | collective-permute-start | bytes 344072 | tf_op jit(solution)/shard_map/ppermute | solution.py:685
  31.7 0.7 copy-start.6
  31.7 0.7 copy-start.7
  56.4 22.1 %collective-permute-start.6 = (f32[320,128]{1,0:T(8,128)S(1)}, f32[320,128]{1,0:T(8,128)S(1)}, u32[]{:S(2)}, u32[]{:S(2)}) collective-permute-start(f32[320,128]{1,0:T(8,128)S(1)} %get-tuple-element.27), channel_id=1, source_target_pairs={{0,1},{1,0},{2,3},{3,2},{4,5},{5,4},{6,7},{7,6},{8,9},{9,8},{10,11... | collective-permute-start | bytes 491528 | tf_op jit(solution)/shard_map/ppermute | solution.py:760
  56.8 21.6 %collective-permute-start.7 = (f32[320,128]{1,0:T(8,128)}, f32[320,128]{1,0:T(8,128)S(1)}, u32[]{:S(2)}, u32[]{:S(2)}) collective-permute-start(f32[320,128]{1,0:T(8,128)} %get-tuple-element.28), channel_id=1, source_target_pairs={{1,2},{2,1},{3,4},{4,3},{5,6},{6,5},{7,127},{9,10},{10,9},{11,12},... | collective-permute-start | bytes 491528 | tf_op jit(solution)/shard_map/ppermute | solution.py:759
  57.5 20.9 %all-to-all-start.1 = ((f32[128,1,256]{2,1,0:T(1,128)}), f32[128,1,256]{2,1,0:T(1,128)S(1)}, u32[]{:S(2)}, u32[]{:S(2)}) async-start(f32[128,1,256]{2,1,0:T(1,128)} %bitcast.9), calls=%async_computation.1 | async-start | bytes 262144 | tf_op jit(solution)/shard_map/all_to_all | solution.py:661
  68.5 4.6 %collective-permute-start.5 = (f32[5,32,128]{2,1,0:T(8,128)S(1)}, f32[5,32,128]{2,1,0:T(8,128)S(1)}, u32[]{:S(2)}, u32[]{:S(2)}) collective-permute-start(f32[5,32,128]{2,1,0:T(8,128)S(1)} %get-tuple-element.26), channel_id=1, source_target_pairs={{8,0},{16,8},{24,16},{32,24},{40,32},{48,40},{56,48},{64,56},{72,6... | collective-permute-start | bytes 245768 | tf_op jit(solution)/shard_map/ppermute | solution.py:685
  69.7 3.8 %collective-permute-start.4 = (f32[5,32,128]{2,1,0:T(8,128)S(1)}, f32[5,32,128]{2,1,0:T(8,128)S(1)}, u32[]{:S(2)}, u32[]{:S(2)}) collective-permute-start(f32[5,32,128]{2,1,0:T(8,128)S(1)} %get-tuple-element.26), channel_id=1, source_target_pairs={{0,8},{8,16},{16,24},{24,32},{32,40},{40,48},{48,56},{56,64},{64,7... | collective-permute-start | bytes 245768 | tf_op jit(solution)/shard_map/ppermute | solution.py:685

commit v2 on v1

--- a/solution.py
+++ b/solution.py
@@ -736,6 +736,7 @@
             (V, from_east),
         ],
         "core",
+        vmem=52,
         scratch=[
             V((padded, CW), f32),
             V((padded, CW), f32),

time: 82.7 us -> 81.1 us (0.981)
  no operation moved by 1% of the time
where the time goes in v2:
time: 81.1 us; the launch traced here: 80.9 us
  Pallas kernels  32.8 us (40%)
  starting transfers between devices  31.2 us (38%)
  waiting for transfers between devices  16.1 us (20%)
    pallas_call x4, Pallas kernels, call(): pl.pallas_call(body, out_shape=[jax.ShapeDtypeStruct(shape, dtype) for sh...  32.8 us
    all_to_all x2, starting transfers between devices, all_to_all(): lax.all_to_all(x, ('lon', 'lat'), split_axis=0, concat_axis=0, tiled=True)  23.4 us
    all_to_all x2, waiting for transfers between devices, all_to_all(): lax.all_to_all(x, ('lon', 'lat'), split_axis=0, concat_axis=0, tiled=True)  9.13 us
    ppermute x4, waiting for transfers between devices, around(): return (lax.ppermute(x, 'lon', eastward), lax.ppermute(x, 'lon', westward))  6.91 us
    ppermute x4, starting transfers between devices, around(): return (lax.ppermute(x, 'lon', eastward), lax.ppermute(x, 'lon', westward))  3.81 us
    ppermute x1, starting transfers between devices, shards(): got1 = lax.ppermute(pay1, both, pairs1)  2.12 us
  transfers between devices with their start and end apart: 10, of which 6 were waited for; matrix products, arithmetic and copies ran while one was open for 0% of the time, Pallas kernels for 0%

profile of v2, /device:TPU:1, one launch (start us, length us, event | category | flops | bytes accessed | tf_op | source)
XLA Modules:
  0.0 80.9 jit_solution(17625274727017564601)
XLA Ops:
  0.6 0.0 copy-start.3
  0.6 0.0 copy-start.4
  0.7 0.0 copy-start
  0.7 0.0 copy-start.2
  0.7 0.0 copy-start.1
  0.7 0.0 copy-start.5
  0.7 2.8 %edges.1 = (f32[7,32,128]{2,1,0:T(8,128)S(1)}, f32[384,128]{1,0:T(8,128)S(1)}, f32[384,128]{1,0:T(8,128)S(1)}) custom-call(f32[5120,128]{1,0:T(8,128)} %bitcast.20, f32[2048,128]{1,0:T(8,128)} %bitcast.22), custom_call_target="tpu_custom_call" | custom-call | flops 1000000 | bytes 1000000 | tf_op jit(solution)/shard_map/edges/pallas_call | solution.py:36
  3.5 0.0 copy-done.3
  3.5 0.0 copy-done.4
  3.5 2.9 %pack.1 = (f32[256,128]{1,0:T(8,128)}, f32[8,128]{1,0:T(8,128)S(1)}) custom-call(s32[1,8]{1,0:T(1,128)S(1)} %copy-done.4, f32[8,128]{1,0:T(8,128)S(1)} %bitcast.17, f32[8,128]{1,0:T(8,128)S(1)} %bitcast.18, s32[8,128]{1,0:T(8,128)S(1)} %bitcast.15, s32[8,128]{1,0:T(8,128)S(1)} %bitcast.19, f32[7,32,128]{2,1,0:T(8,128)S(1)} %get-tuple-element.19.own), custom_call_target="tpu_custom_call" | custom-call | flops 1000000 | bytes 1000000 | tf_op jit(solution)/shard_map/pack/pallas_call | solution.py:36
  6.4 2.1 %collective-permute-start = (f32[384,128]{1,0:T(8,128)S(1)}, f32[384,128]{1,0:T(8,128)S(1)}, u32[]{:S(2)}, u32[]{:S(2)}) collective-permute-start(f32[384,128]{1,0:T(8,128)S(1)} %get-tuple-element.22), channel_id=1, source_target_pairs={{0,1},{1,0},{2,3},{3,2},{4,5},{5,4},{6,7},{7,6},{8,9},{9,8},{10,11... | collective-permute-start | bytes 589832 | tf_op jit(solution)/shard_map/ppermute | solution.py:714
  8.6 0.7 collective-permute-start.1
  9.2 12.5 %all-to-all-start = ((f32[128,1,256]{2,1,0:T(1,128)}), f32[128,1,256]{2,1,0:T(1,128)S(1)}, u32[]{:S(2)}, u32[]{:S(2)}) async-start(f32[128,1,256]{2,1,0:T(1,128)} %bitcast.6), calls=%async_computation | async-start | bytes 262144 | tf_op jit(solution)/shard_map/all_to_all | solution.py:661
  21.8 1.1 %collective-permute-start.3 = (f32[7,32,128]{2,1,0:T(8,128)S(1)}, f32[7,32,128]{2,1,0:T(8,128)S(1)}, u32[]{:S(2)}, u32[]{:S(2)}) collective-permute-start(f32[7,32,128]{2,1,0:T(8,128)S(1)} %get-tuple-element.19.own), channel_id=1, source_target_pairs={{8,0},{16,8},{24,16},{32,24},{40,32},{48,40},{56,48},{64,56},{72,6... | collective-permute-start | bytes 344072 | tf_op jit(solution)/shard_map/ppermute | solution.py:685
  22.9 0.8 collective-permute-start.2
  23.7 3.2 %collective-permute-done.3.from_east = f32[7,32,128]{2,1,0:T(8,128)S(1)} collective-permute-done((f32[7,32,128]{2,1,0:T(8,128)S(1)}, f32[7,32,128]{2,1,0:T(8,128)S(1)}, u32[]{:S(2)}, u32[]{:S(2)}) %collective-permute-start.3) | collective-permute-done | bytes 114720 | tf_op jit(solution)/shard_map/ppermute | solution.py:685
  26.8 0.8 collective-permute-done.2.from_west
  27.6 4.1 %all-to-all-done = f32[128,1,256]{2,1,0:T(1,128)S(1)} async-done(((f32[128,1,256]{2,1,0:T(1,128)}), f32[128,1,256]{2,1,0:T(1,128)S(1)}, u32[]{:S(2)}, u32[]{:S(2)}) %all-to-all-start) | async-done | bytes 131104 | tf_op jit(solution)/shard_map/all_to_all | solution.py:661
  31.7 0.0 collective-permute-done.got1
  31.7 0.0 collective-permute-done.1.got2
  31.7 23.2 %core.1 = (f32[256,128]{1,0:T(8,128)}, f32[5120,128]{1,0:T(8,128)}, f32[5120,128]{1,0:T(8,128)}, f32[320,128]{1,0:T(8,128)S(1)}, f32[320,128]{1,0:T(8,128)S(1)}, /*index=5*/f32[5,32,128]{2,1,0:T(8,128)S(1)}) custom-call(f32[5]{0:T(128)S(1)} %copy-done.5, f32[256,128]{1,0:T(8,128)S(1)} %bitcast.13, f32[5120,128]{1,0:T(8,128)} %bitcast.21, ...), custom_call_target="tpu_custom_call" | custom-call | flops 1000000 | bytes 1000000 | tf_op jit(solution)/shard_map/core/pallas_call | solution.py:36
  54.9 0.5 collective-permute-start.6
  55.4 0.7 collective-permute-start.7
  56.1 10.9 %all-to-all-start.1 = ((f32[128,1,256]{2,1,0:T(1,128)}), f32[128,1,256]{2,1,0:T(1,128)S(1)}, u32[]{:S(2)}, u32[]{:S(2)}) async-start(f32[128,1,256]{2,1,0:T(1,128)} %bitcast.9), calls=%async_computation.1 | async-start | bytes 262144 | tf_op jit(solution)/shard_map/all_to_all | solution.py:661
  67.0 1.1 %collective-permute-start.5 = (f32[5,32,128]{2,1,0:T(8,128)S(1)}, f32[5,32,128]{2,1,0:T(8,128)S(1)}, u32[]{:S(2)}, u32[]{:S(2)}) collective-permute-start(f32[5,32,128]{2,1,0:T(8,128)S(1)} %get-tuple-element.26), channel_id=1, source_target_pairs={{8,0},{16,8},{24,16},{32,24},{40,32},{48,40},{56,48},{64,56},{72,6... | collective-permute-start | bytes 245768 | tf_op jit(solution)/shard_map/ppermute | solution.py:685
  68.1 0.8 collective-permute-start.4
  68.9 2.7 %collective-permute-done.5.from_east = f32[5,32,128]{2,1,0:T(8,128)S(1)} collective-permute-done((f32[5,32,128]{2,1,0:T(8,128)S(1)}, f32[5,32,128]{2,1,0:T(8,128)S(1)}, u32[]{:S(2)}, u32[]{:S(2)}) %collective-permute-start.5) | collective-permute-done | bytes 81952 | tf_op jit(solution)/shard_map/ppermute | solution.py:685
  71.6 0.3 collective-permute-done.4.from_west
  71.9 5.0 %all-to-all-done.1 = f32[128,1,256]{2,1,0:T(1,128)S(1)} async-done(((f32[128,1,256]{2,1,0:T(1,128)}), f32[128,1,256]{2,1,0:T(1,128)S(1)}, u32[]{:S(2)}, u32[]{:S(2)}) %all-to-all-start.1) | async-done | bytes 131104 | tf_op jit(solution)/shard_map/all_to_all | solution.py:661
  76.9 0.0 collective-permute-done.6.got1
  76.9 0.0 collective-permute-done.7.got2
  76.9 4.0 %finish.1 = (f32[5120,128]{1,0:T(8,128)}, f32[8,128]{1,0:T(8,128)}) custom-call(f32[5120,128]{1,0:T(8,128)} %get-tuple-element.25.part, f32[5,32,128]{2,1,0:T(8,128)S(1)} %collective-permute-done.4.from_west, f32[5,32,128]{2,1,0:T(8,128)S(1)} %collective-permute-done.5.from_east, f32[320,128]{1,0:T(8,128)S(1)} %collective-permute-done.6.got1, ...), custom_call_target="tpu_custom_call" | custom-call | flops 1000000 | bytes 1000000 | tf_op jit(solution)/shard_map/finish/pallas_call | solution.py:36
  (4 shorter events, 0.0 us)
Async XLA Ops:
  0.6 2.8 %copy-start.3 = (s32[1024]{0:T(1024)S(1)}, s32[1024]{0:T(1024)}, u32[]{:S(2)}) copy-start(s32[1024]{0:T(1024)} %param.15) | copy-start | bytes 12292
  0.6 2.8 %copy-start.4 = (s32[1,8]{1,0:T(1,128)S(1)}, s32[1,8]{1,0:T(1,128)}, u32[]{:S(2)}) copy-start(s32[1,8]{1,0:T(1,128)} %counts.1) | copy-start | bytes 100
  0.7 2.8 %copy-start = (s32[1024,1]{0,1:T(1,128)S(1)}, s32[1024,1]{0,1:T(1,128)}, u32[]{:S(2)}) copy-start(s32[1024,1]{0,1:T(1,128)} %param.13) | copy-start | bytes 12292
  0.7 2.8 %copy-start.2 = (f32[1024]{0:T(1024)S(1)}, f32[1024]{0:T(1024)}, u32[]{:S(2)}) copy-start(f32[1024]{0:T(1024)} %param.12) | copy-start | bytes 12292
  0.7 2.8 %copy-start.1 = (f32[1024]{0:T(1024)S(1)}, f32[1024]{0:T(1024)}, u32[]{:S(2)}) copy-start(f32[1024]{0:T(1024)} %param.11) | copy-start | bytes 12292
  0.7 31.0 %copy-start.5 = (f32[5]{0:T(128)S(1)}, f32[5]{0:T(128)}, u32[]{:S(2)}) copy-start(f32[5]{0:T(128)} %kap.1) | copy-start | bytes 64
  6.4 25.3 %collective-permute-start = (f32[384,128]{1,0:T(8,128)S(1)}, f32[384,128]{1,0:T(8,128)S(1)}, u32[]{:S(2)}, u32[]{:S(2)}) collective-permute-start(f32[384,128]{1,0:T(8,128)S(1)} %get-tuple-element.22), channel_id=1, source_target_pairs={{0,1},{1,0},{2,3},{3,2},{4,5},{5,4},{6,7},{7,6},{8,9},{9,8},{10,11... | collective-permute-start | bytes 589832 | tf_op jit(solution)/shard_map/ppermute | solution.py:714
  8.6 23.1 %collective-permute-start.1 = (f32[384,128]{1,0:T(8,128)S(1)}, f32[384,128]{1,0:T(8,128)S(1)}, u32[]{:S(2)}, u32[]{:S(2)}) collective-permute-start(f32[384,128]{1,0:T(8,128)S(1)} %get-tuple-element.23), channel_id=1, source_target_pairs={{1,2},{2,1},{3,4},{4,3},{5,6},{6,5},{7,127},{9,10},{10,9},{11,12},... | collective-permute-start | bytes 589832 | tf_op jit(solution)/shard_map/ppermute | solution.py:696
  9.2 22.5 %all-to-all-start = ((f32[128,1,256]{2,1,0:T(1,128)}), f32[128,1,256]{2,1,0:T(1,128)S(1)}, u32[]{:S(2)}, u32[]{:S(2)}) async-start(f32[128,1,256]{2,1,0:T(1,128)} %bitcast.6), calls=%async_computation | async-start | bytes 262144 | tf_op jit(solution)/shard_map/all_to_all | solution.py:661
  21.8 5.1 %collective-permute-start.3 = (f32[7,32,128]{2,1,0:T(8,128)S(1)}, f32[7,32,128]{2,1,0:T(8,128)S(1)}, u32[]{:S(2)}, u32[]{:S(2)}) collective-permute-start(f32[7,32,128]{2,1,0:T(8,128)S(1)} %get-tuple-element.19.own), channel_id=1, source_target_pairs={{8,0},{16,8},{24,16},{32,24},{40,32},{48,40},{56,48},{64,56},{72,6... | collective-permute-start | bytes 344072 | tf_op jit(solution)/shard_map/ppermute | solution.py:685
  22.9 4.7 %collective-permute-start.2 = (f32[7,32,128]{2,1,0:T(8,128)S(1)}, f32[7,32,128]{2,1,0:T(8,128)S(1)}, u32[]{:S(2)}, u32[]{:S(2)}) collective-permute-start(f32[7,32,128]{2,1,0:T(8,128)S(1)} %get-tuple-element.19.own), channel_id=1, source_target_pairs={{0,8},{8,16},{16,24},{24,32},{32,40},{40,48},{48,56},{56,64},{64,7... | collective-permute-start | bytes 344072 | tf_op jit(solution)/shard_map/ppermute | solution.py:685
  54.9 22.0 %collective-permute-start.6 = (f32[320,128]{1,0:T(8,128)S(1)}, f32[320,128]{1,0:T(8,128)S(1)}, u32[]{:S(2)}, u32[]{:S(2)}) collective-permute-start(f32[320,128]{1,0:T(8,128)S(1)} %get-tuple-element.27), channel_id=1, source_target_pairs={{0,1},{1,0},{2,3},{3,2},{4,5},{5,4},{6,7},{7,6},{8,9},{9,8},{10,11... | collective-permute-start | bytes 491528 | tf_op jit(solution)/shard_map/ppermute | solution.py:761
  55.4 21.5 %collective-permute-start.7 = (f32[320,128]{1,0:T(8,128)S(1)}, f32[320,128]{1,0:T(8,128)S(1)}, u32[]{:S(2)}, u32[]{:S(2)}) collective-permute-start(f32[320,128]{1,0:T(8,128)S(1)} %get-tuple-element.28), channel_id=1, source_target_pairs={{1,2},{2,1},{3,4},{4,3},{5,6},{6,5},{7,127},{9,10},{10,9},{11,12},... | collective-permute-start | bytes 491528 | tf_op jit(solution)/shard_map/ppermute | solution.py:760
  56.1 20.8 %all-to-all-start.1 = ((f32[128,1,256]{2,1,0:T(1,128)}), f32[128,1,256]{2,1,0:T(1,128)S(1)}, u32[]{:S(2)}, u32[]{:S(2)}) async-start(f32[128,1,256]{2,1,0:T(1,128)} %bitcast.9), calls=%async_computation.1 | async-start | bytes 262144 | tf_op jit(solution)/shard_map/all_to_all | solution.py:661
  67.0 4.6 %collective-permute-start.5 = (f32[5,32,128]{2,1,0:T(8,128)S(1)}, f32[5,32,128]{2,1,0:T(8,128)S(1)}, u32[]{:S(2)}, u32[]{:S(2)}) collective-permute-start(f32[5,32,128]{2,1,0:T(8,128)S(1)} %get-tuple-element.26), channel_id=1, source_target_pairs={{8,0},{16,8},{24,16},{32,24},{40,32},{48,40},{56,48},{64,56},{72,6... | collective-permute-start | bytes 245768 | tf_op jit(solution)/shard_map/ppermute | solution.py:685
  68.1 3.8 %collective-permute-start.4 = (f32[5,32,128]{2,1,0:T(8,128)S(1)}, f32[5,32,128]{2,1,0:T(8,128)S(1)}, u32[]{:S(2)}, u32[]{:S(2)}) collective-permute-start(f32[5,32,128]{2,1,0:T(8,128)S(1)} %get-tuple-element.26), channel_id=1, source_target_pairs={{0,8},{8,16},{16,24},{24,32},{32,40},{40,48},{48,56},{56,64},{64,7... | collective-permute-start | bytes 245768 | tf_op jit(solution)/shard_map/ppermute | solution.py:685

commit v3 on v2

--- a/solution.py
+++ b/solution.py
@@ -259,7 +259,7 @@
 
 PAD = 8
 GROUP = 8
-UNROLL = 8
+UNROLL = 16
 TILES = CL // 8
 
 
@@ -401,7 +401,7 @@
 
     load_i.wait()
 
-    @pl.loop(0, NDEV, unroll=4)
+    @pl.loop(0, NDEV, unroll=8)
     def _(s):
         for q in range(CAP):
             at = index_s[q, s]
@@ -438,7 +438,7 @@
                 acc = acc + jnp.where(mine == cell_of[other, :] >> 7, adds[other, :], 0.0)
             adds[cut, :] = acc
 
-    @pl.loop(0, NDEV, unroll=4)
+    @pl.loop(0, NDEV, unroll=8)
     def _(s):
         for start in range(0, CAP, GROUP):
             ats = [index_s[q, s] for q in range(start, start + GROUP)]

time: 81.1 us -> 80.4 us (level)
  Pallas kernels: 32.8 us -> 31.9 us
    pallas_call x4, Pallas kernels: 32.8 us -> 31.9 us  [call(): pl.pallas_call(body, out_shape=[jax.ShapeDtypeStruct(shape, dtype) for sh...]
where the time goes in v3:
time: 80.4 us; the launch traced here: 80.2 us
  Pallas kernels  31.9 us (40%)
  starting transfers between devices  31.2 us (39%)
  waiting for transfers between devices  16.1 us (20%)
  between operations  0.94 us (1%)
    pallas_call x4, Pallas kernels, call(): pl.pallas_call(body, out_shape=[jax.ShapeDtypeStruct(shape, dtype) for sh...  31.9 us
    all_to_all x2, starting transfers between devices, all_to_all(): lax.all_to_all(x, ('lon', 'lat'), split_axis=0, concat_axis=0, tiled=True)  23.5 us
    all_to_all x2, waiting for transfers between devices, all_to_all(): lax.all_to_all(x, ('lon', 'lat'), split_axis=0, concat_axis=0, tiled=True)  9.13 us
    ppermute x4, waiting for transfers between devices, around(): return (lax.ppermute(x, 'lon', eastward), lax.ppermute(x, 'lon', westward))  6.91 us
    ppermute x4, starting transfers between devices, around(): return (lax.ppermute(x, 'lon', eastward), lax.ppermute(x, 'lon', westward))  3.81 us
    ppermute x1, starting transfers between devices, shards(): got1 = lax.ppermute(pay1, both, pairs1)  2.13 us
  transfers between devices with their start and end apart: 10, of which 6 were waited for; matrix products, arithmetic and copies ran while one was open for 0% of the time, Pallas kernels for 0%

profile of v3, /device:TPU:1, one launch (start us, length us, event | category | flops | bytes accessed | tf_op | source)
XLA Modules:
  0.0 80.2 jit_solution(7465137214859662488)
XLA Ops:
  0.6 0.0 copy-start.3
  0.6 0.0 copy-start.4
  0.7 0.0 copy-start
  0.7 0.0 copy-start.2
  0.7 0.0 copy-start.1
  0.7 0.0 copy-start.5
  0.7 2.8 %edges.1 = (f32[7,32,128]{2,1,0:T(8,128)S(1)}, f32[384,128]{1,0:T(8,128)S(1)}, f32[384,128]{1,0:T(8,128)S(1)}) custom-call(f32[5120,128]{1,0:T(8,128)} %bitcast.20, f32[2048,128]{1,0:T(8,128)} %bitcast.22), custom_call_target="tpu_custom_call" | custom-call | flops 1000000 | bytes 1000000 | tf_op jit(solution)/shard_map/edges/pallas_call | solution.py:36
  3.5 0.0 copy-done.3
  3.5 2.9 %pack.1 = (f32[256,128]{1,0:T(8,128)}, f32[8,128]{1,0:T(8,128)S(1)}) custom-call(s32[1,8]{1,0:T(1,128)S(1)} %copy-done.4, f32[8,128]{1,0:T(8,128)S(1)} %bitcast.17, f32[8,128]{1,0:T(8,128)S(1)} %bitcast.18, s32[8,128]{1,0:T(8,128)S(1)} %bitcast.15, s32[8,128]{1,0:T(8,128)S(1)} %bitcast.19, f32[7,32,128]{2,1,0:T(8,128)S(1)} %get-tuple-element.19.own), custom_call_target="tpu_custom_call" | custom-call | flops 1000000 | bytes 1000000 | tf_op jit(solution)/shard_map/pack/pallas_call | solution.py:36
  6.4 2.1 %collective-permute-start = (f32[384,128]{1,0:T(8,128)S(1)}, f32[384,128]{1,0:T(8,128)S(1)}, u32[]{:S(2)}, u32[]{:S(2)}) collective-permute-start(f32[384,128]{1,0:T(8,128)S(1)} %get-tuple-element.22), channel_id=1, source_target_pairs={{0,1},{1,0},{2,3},{3,2},{4,5},{5,4},{6,7},{7,6},{8,9},{9,8},{10,11... | collective-permute-start | bytes 589832 | tf_op jit(solution)/shard_map/ppermute | solution.py:714
  8.6 0.7 collective-permute-start.1
  9.2 12.5 %all-to-all-start = ((f32[128,1,256]{2,1,0:T(1,128)}), f32[128,1,256]{2,1,0:T(1,128)S(1)}, u32[]{:S(2)}, u32[]{:S(2)}) async-start(f32[128,1,256]{2,1,0:T(1,128)} %bitcast.6), calls=%async_computation | async-start | bytes 262144 | tf_op jit(solution)/shard_map/all_to_all | solution.py:661
  21.8 1.1 %collective-permute-start.3 = (f32[7,32,128]{2,1,0:T(8,128)S(1)}, f32[7,32,128]{2,1,0:T(8,128)S(1)}, u32[]{:S(2)}, u32[]{:S(2)}) collective-permute-start(f32[7,32,128]{2,1,0:T(8,128)S(1)} %get-tuple-element.19.own), channel_id=1, source_target_pairs={{8,0},{16,8},{24,16},{32,24},{40,32},{48,40},{56,48},{64,56},{72,6... | collective-permute-start | bytes 344072 | tf_op jit(solution)/shard_map/ppermute | solution.py:685
  22.9 0.8 collective-permute-start.2
  23.7 3.2 %collective-permute-done.3.from_east = f32[7,32,128]{2,1,0:T(8,128)S(1)} collective-permute-done((f32[7,32,128]{2,1,0:T(8,128)S(1)}, f32[7,32,128]{2,1,0:T(8,128)S(1)}, u32[]{:S(2)}, u32[]{:S(2)}) %collective-permute-start.3) | collective-permute-done | bytes 114720 | tf_op jit(solution)/shard_map/ppermute | solution.py:685
  26.8 0.8 collective-permute-done.2.from_west
  27.6 4.1 %all-to-all-done = f32[128,1,256]{2,1,0:T(1,128)S(1)} async-done(((f32[128,1,256]{2,1,0:T(1,128)}), f32[128,1,256]{2,1,0:T(1,128)S(1)}, u32[]{:S(2)}, u32[]{:S(2)}) %all-to-all-start) | async-done | bytes 131104 | tf_op jit(solution)/shard_map/all_to_all | solution.py:661
  31.7 0.0 collective-permute-done.got1
  31.7 0.0 collective-permute-done.1.got2
  31.7 0.0 copy-done.5
  31.7 22.3 %core.1 = (f32[256,128]{1,0:T(8,128)}, f32[5120,128]{1,0:T(8,128)}, f32[5120,128]{1,0:T(8,128)}, f32[320,128]{1,0:T(8,128)S(1)}, f32[320,128]{1,0:T(8,128)S(1)}, /*index=5*/f32[5,32,128]{2,1,0:T(8,128)S(1)}) custom-call(f32[5]{0:T(128)S(1)} %copy-done.5, f32[256,128]{1,0:T(8,128)S(1)} %bitcast.13, f32[5120,128]{1,0:T(8,128)} %bitcast.21, ...), custom_call_target="tpu_custom_call" | custom-call | flops 1000000 | bytes 1000000 | tf_op jit(solution)/shard_map/core/pallas_call | solution.py:36
  54.0 0.5 collective-permute-start.6
  54.4 0.7 collective-permute-start.7
  55.1 11.0 %all-to-all-start.1 = ((f32[128,1,256]{2,1,0:T(1,128)}), f32[128,1,256]{2,1,0:T(1,128)S(1)}, u32[]{:S(2)}, u32[]{:S(2)}) async-start(f32[128,1,256]{2,1,0:T(1,128)} %bitcast.9), calls=%async_computation.1 | async-start | bytes 262144 | tf_op jit(solution)/shard_map/all_to_all | solution.py:661
  66.1 1.1 %collective-permute-start.5 = (f32[5,32,128]{2,1,0:T(8,128)S(1)}, f32[5,32,128]{2,1,0:T(8,128)S(1)}, u32[]{:S(2)}, u32[]{:S(2)}) collective-permute-start(f32[5,32,128]{2,1,0:T(8,128)S(1)} %get-tuple-element.26), channel_id=1, source_target_pairs={{8,0},{16,8},{24,16},{32,24},{40,32},{48,40},{56,48},{64,56},{72,6... | collective-permute-start | bytes 245768 | tf_op jit(solution)/shard_map/ppermute | solution.py:685
  67.2 0.8 collective-permute-start.4
  68.0 2.7 %collective-permute-done.5.from_east = f32[5,32,128]{2,1,0:T(8,128)S(1)} collective-permute-done((f32[5,32,128]{2,1,0:T(8,128)S(1)}, f32[5,32,128]{2,1,0:T(8,128)S(1)}, u32[]{:S(2)}, u32[]{:S(2)}) %collective-permute-start.5) | collective-permute-done | bytes 81952 | tf_op jit(solution)/shard_map/ppermute | solution.py:685
  70.7 0.3 collective-permute-done.4.from_west
  71.0 5.0 %all-to-all-done.1 = f32[128,1,256]{2,1,0:T(1,128)S(1)} async-done(((f32[128,1,256]{2,1,0:T(1,128)}), f32[128,1,256]{2,1,0:T(1,128)S(1)}, u32[]{:S(2)}, u32[]{:S(2)}) %all-to-all-start.1) | async-done | bytes 131104 | tf_op jit(solution)/shard_map/all_to_all | solution.py:661
  76.0 0.0 collective-permute-done.6.got1
  76.0 0.0 collective-permute-done.7.got2
  76.0 4.0 %finish.1 = (f32[5120,128]{1,0:T(8,128)}, f32[8,128]{1,0:T(8,128)}) custom-call(f32[5120,128]{1,0:T(8,128)} %get-tuple-element.25.part, f32[5,32,128]{2,1,0:T(8,128)S(1)} %collective-permute-done.4.from_west, f32[5,32,128]{2,1,0:T(8,128)S(1)} %collective-permute-done.5.from_east, f32[320,128]{1,0:T(8,128)S(1)} %collective-permute-done.6.got1, ...), custom_call_target="tpu_custom_call" | custom-call | flops 1000000 | bytes 1000000 | tf_op jit(solution)/shard_map/finish/pallas_call | solution.py:36
  (4 shorter events, 0.0 us)
Async XLA Ops:
  0.6 2.8 %copy-start.3 = (s32[1024]{0:T(1024)S(1)}, s32[1024]{0:T(1024)}, u32[]{:S(2)}) copy-start(s32[1024]{0:T(1024)} %param.15) | copy-start | bytes 12292
  0.6 2.8 %copy-start.4 = (s32[1,8]{1,0:T(1,128)S(1)}, s32[1,8]{1,0:T(1,128)}, u32[]{:S(2)}) copy-start(s32[1,8]{1,0:T(1,128)} %counts.1) | copy-start | bytes 100
  0.7 2.8 %copy-start = (s32[1024,1]{0,1:T(1,128)S(1)}, s32[1024,1]{0,1:T(1,128)}, u32[]{:S(2)}) copy-start(s32[1024,1]{0,1:T(1,128)} %param.13) | copy-start | bytes 12292
  0.7 2.8 %copy-start.2 = (f32[1024]{0:T(1024)S(1)}, f32[1024]{0:T(1024)}, u32[]{:S(2)}) copy-start(f32[1024]{0:T(1024)} %param.12) | copy-start | bytes 12292
  0.7 2.8 %copy-start.1 = (f32[1024]{0:T(1024)S(1)}, f32[1024]{0:T(1024)}, u32[]{:S(2)}) copy-start(f32[1024]{0:T(1024)} %param.11) | copy-start | bytes 12292
  0.7 31.0 %copy-start.5 = (f32[5]{0:T(128)S(1)}, f32[5]{0:T(128)}, u32[]{:S(2)}) copy-start(f32[5]{0:T(128)} %kap.1) | copy-start | bytes 64
  6.4 25.3 %collective-permute-start = (f32[384,128]{1,0:T(8,128)S(1)}, f32[384,128]{1,0:T(8,128)S(1)}, u32[]{:S(2)}, u32[]{:S(2)}) collective-permute-start(f32[384,128]{1,0:T(8,128)S(1)} %get-tuple-element.22), channel_id=1, source_target_pairs={{0,1},{1,0},{2,3},{3,2},{4,5},{5,4},{6,7},{7,6},{8,9},{9,8},{10,11... | collective-permute-start | bytes 589832 | tf_op jit(solution)/shard_map/ppermute | solution.py:714
  8.6 23.1 %collective-permute-start.1 = (f32[384,128]{1,0:T(8,128)S(1)}, f32[384,128]{1,0:T(8,128)S(1)}, u32[]{:S(2)}, u32[]{:S(2)}) collective-permute-start(f32[384,128]{1,0:T(8,128)S(1)} %get-tuple-element.23), channel_id=1, source_target_pairs={{1,2},{2,1},{3,4},{4,3},{5,6},{6,5},{7,127},{9,10},{10,9},{11,12},... | collective-permute-start | bytes 589832 | tf_op jit(solution)/shard_map/ppermute | solution.py:696
  9.2 22.5 %all-to-all-start = ((f32[128,1,256]{2,1,0:T(1,128)}), f32[128,1,256]{2,1,0:T(1,128)S(1)}, u32[]{:S(2)}, u32[]{:S(2)}) async-start(f32[128,1,256]{2,1,0:T(1,128)} %bitcast.6), calls=%async_computation | async-start | bytes 262144 | tf_op jit(solution)/shard_map/all_to_all | solution.py:661
  21.8 5.1 %collective-permute-start.3 = (f32[7,32,128]{2,1,0:T(8,128)S(1)}, f32[7,32,128]{2,1,0:T(8,128)S(1)}, u32[]{:S(2)}, u32[]{:S(2)}) collective-permute-start(f32[7,32,128]{2,1,0:T(8,128)S(1)} %get-tuple-element.19.own), channel_id=1, source_target_pairs={{8,0},{16,8},{24,16},{32,24},{40,32},{48,40},{56,48},{64,56},{72,6... | collective-permute-start | bytes 344072 | tf_op jit(solution)/shard_map/ppermute | solution.py:685
  22.9 4.7 %collective-permute-start.2 = (f32[7,32,128]{2,1,0:T(8,128)S(1)}, f32[7,32,128]{2,1,0:T(8,128)S(1)}, u32[]{:S(2)}, u32[]{:S(2)}) collective-permute-start(f32[7,32,128]{2,1,0:T(8,128)S(1)} %get-tuple-element.19.own), channel_id=1, source_target_pairs={{0,8},{8,16},{16,24},{24,32},{32,40},{40,48},{48,56},{56,64},{64,7... | collective-permute-start | bytes 344072 | tf_op jit(solution)/shard_map/ppermute | solution.py:685
  54.0 22.1 %collective-permute-start.6 = (f32[320,128]{1,0:T(8,128)S(1)}, f32[320,128]{1,0:T(8,128)S(1)}, u32[]{:S(2)}, u32[]{:S(2)}) collective-permute-start(f32[320,128]{1,0:T(8,128)S(1)} %get-tuple-element.27), channel_id=1, source_target_pairs={{0,1},{1,0},{2,3},{3,2},{4,5},{5,4},{6,7},{7,6},{8,9},{9,8},{10,11... | collective-permute-start | bytes 491528 | tf_op jit(solution)/shard_map/ppermute | solution.py:761
  54.4 21.6 %collective-permute-start.7 = (f32[320,128]{1,0:T(8,128)S(1)}, f32[320,128]{1,0:T(8,128)S(1)}, u32[]{:S(2)}, u32[]{:S(2)}) collective-permute-start(f32[320,128]{1,0:T(8,128)S(1)} %get-tuple-element.28), channel_id=1, source_target_pairs={{1,2},{2,1},{3,4},{4,3},{5,6},{6,5},{7,127},{9,10},{10,9},{11,12},... | collective-permute-start | bytes 491528 | tf_op jit(solution)/shard_map/ppermute | solution.py:760
  55.1 20.9 %all-to-all-start.1 = ((f32[128,1,256]{2,1,0:T(1,128)}), f32[128,1,256]{2,1,0:T(1,128)S(1)}, u32[]{:S(2)}, u32[]{:S(2)}) async-start(f32[128,1,256]{2,1,0:T(1,128)} %bitcast.9), calls=%async_computation.1 | async-start | bytes 262144 | tf_op jit(solution)/shard_map/all_to_all | solution.py:661
  66.1 4.6 %collective-permute-start.5 = (f32[5,32,128]{2,1,0:T(8,128)S(1)}, f32[5,32,128]{2,1,0:T(8,128)S(1)}, u32[]{:S(2)}, u32[]{:S(2)}) collective-permute-start(f32[5,32,128]{2,1,0:T(8,128)S(1)} %get-tuple-element.26), channel_id=1, source_target_pairs={{8,0},{16,8},{24,16},{32,24},{40,32},{48,40},{56,48},{64,56},{72,6... | collective-permute-start | bytes 245768 | tf_op jit(solution)/shard_map/ppermute | solution.py:685
  67.2 3.8 %collective-permute-start.4 = (f32[5,32,128]{2,1,0:T(8,128)S(1)}, f32[5,32,128]{2,1,0:T(8,128)S(1)}, u32[]{:S(2)}, u32[]{:S(2)}) collective-permute-start(f32[5,32,128]{2,1,0:T(8,128)S(1)} %get-tuple-element.26), channel_id=1, source_target_pairs={{0,8},{8,16},{16,24},{24,32},{32,40},{40,48},{48,56},{56,64},{64,7... | collective-permute-start | bytes 245768 | tf_op jit(solution)/shard_map/ppermute | solution.py:685
